TPU v7x, 512 devices: a whole 4x8x8 slice. The times are simulated.
512 devices in a mesh: dp: 32 (over z, y_lo, core), ctx: 16 (over y_hi, x).
Axes of the slice: x: 4, y: 8 (y_hi: 4, y_lo: 2; y = y_hi * 2 + y_lo), z: 8, core: 2. Of those that a mesh axis runs over, the one named last changes fastest.
Arguments:
- queries: bfloat16 [32, 2048, 4096], P('dp', 'ctx'), may hold values from -8 to 8
- key_rows: bfloat16 [32, 2048, 512], P('dp', 'ctx'), may hold values from -8 to 8
- values: bfloat16 [32, 2048, 512], P('dp', 'ctx'), may hold values from -6 to 6
- outputs: bfloat16 [32, 2048, 4096], P('dp', 'ctx'), may hold values from -4 to 4
- out_grads: bfloat16 [32, 2048, 4096], P('dp', 'ctx'), may hold values from -6 to 6
- depths: int32 [32, 2048], P('dp', 'ctx'), may hold values from 0 to 63, as said below
- subtree_end: int32 [32, 2048], P('dp', 'ctx'), may hold values from 64 to 2048, as said below
- file_lengths: int32 [32, 8], P('dp'), may hold values from 1 to 1536, 2048 in all within a row
- slopes: float32 [32], replicated, may hold values from 0.02 to 0.5
- ancestor_gain: float32 [32], replicated, may hold values from 0.5 to 3
Outputs:
- query_grads: bfloat16 [32, 2048, 4096], P('dp', 'ctx')
- key_grads: bfloat16 [32, 2048, 512], P('dp', 'ctx')
- value_grads: bfloat16 [32, 2048, 512], P('dp', 'ctx')
- bias_grads: float32 [32, 2], P('ctx')
Inputs may be any that keep to these rules, and one draw needn't show every extreme that they name: `depths`: token t has depth t for t < 64; afterwards the depth changes by at most one from a token to the next. `subtree_end`: the first later position of the same sequence whose depth is not above the token's depth, or 2048 where there is none.
All inputs are finite; a program needn't handle non-finite values.
Results may differ from a plain program's by a relative error of at most 0.012.
Values may be sent and summed in bfloat16 or wider, within the bound.
A program may use at most 64 MiB of HBM per device.

v0:
```python
import jax
import jax.numpy as jnp
from jax import lax
from jax.sharding import PartitionSpec as P

HEAD_WIDTH = 128


masked_score = -1e30


def file_index(lengths_row, positions):
    bounds = jnp.cumsum(lengths_row)
    return jnp.sum((positions[:, None] >= bounds[None, :]).astype(jnp.int32), axis=1)


def add_rows(running, update, start_row):
    current = lax.dynamic_slice_in_dim(running, start_row, update.shape[0], 0)
    return lax.dynamic_update_slice_in_dim(running, current + update, start_row, 0)


def body(
    queries,
    key_rows,
    values,
    outputs,
    out_grads,
    depths,
    subtree_end,
    file_lengths,
    slopes,
    ancestor_gain,
):
    tokens_here = queries.shape[1]
    context_size = lax.axis_size("ctx")
    heads_all = queries.shape[2] // HEAD_WIDTH
    kv_heads = key_rows.shape[2] // HEAD_WIDTH
    local_heads = heads_all // context_size
    group_width = heads_all // kv_heads
    repeats = context_size // kv_heads
    seq_len = tokens_here * context_size
    block_rows = min(256, seq_len)
    num_blocks = seq_len // block_rows
    factor = HEAD_WIDTH ** (-0.5)
    head_first = lax.axis_index("ctx") * local_heads
    kv_index = head_first // group_width
    local_slopes = lax.dynamic_slice_in_dim(slopes, head_first, local_heads)
    local_gains = lax.dynamic_slice_in_dim(ancestor_gain, head_first, local_heads)
    depth_whole, end_whole = (
        lax.all_gather(depths, "ctx", axis=1, tiled=True),
        lax.all_gather(subtree_end, "ctx", axis=1, tiled=True),
    )
    depth_whole = depth_whole[0]
    end_whole = end_whole[0]
    positions = jnp.arange(seq_len, dtype=jnp.int32)
    file_whole = file_index(file_lengths[0], positions)
    query_split = queries[0].reshape(tokens_here, context_size, local_heads * HEAD_WIDTH)
    grad_split = out_grads[0].reshape(tokens_here, context_size, local_heads * HEAD_WIDTH)
    output_split = outputs[0].reshape(tokens_here, context_size, local_heads * HEAD_WIDTH)
    query_heads, grad_heads, output_heads = (
        lax.all_to_all(query_split, "ctx", split_axis=1, concat_axis=0, tiled=True),
        lax.all_to_all(grad_split, "ctx", split_axis=1, concat_axis=0, tiled=True),
        lax.all_to_all(output_split, "ctx", split_axis=1, concat_axis=0, tiled=True),
    )
    grad_heads = grad_heads.reshape(seq_len, local_heads, HEAD_WIDTH)
    output_heads = output_heads.reshape(seq_len, local_heads, HEAD_WIDTH)
    row_delta = jnp.sum(grad_heads.astype(jnp.float32) * output_heads.astype(jnp.float32), axis=2)
    query_heads = query_heads.reshape(seq_len, local_heads, HEAD_WIDTH)
    key_whole, value_whole = (
        lax.all_gather(key_rows[0], "ctx", axis=0, tiled=True),
        lax.all_gather(values[0], "ctx", axis=0, tiled=True),
    )
    key_head = lax.dynamic_slice_in_dim(key_whole, kv_index * HEAD_WIDTH, HEAD_WIDTH, 1)
    value_head = lax.dynamic_slice_in_dim(value_whole, kv_index * HEAD_WIDTH, HEAD_WIDTH, 1)

    def tile_block(query_block, key_block, query_start, key_start):
        raw = (
            jnp.einsum("qhe,ke->hqk", query_block, key_block, preferred_element_type=jnp.float32)
            * factor
        )
        query_depth = lax.dynamic_slice_in_dim(depth_whole, query_start, block_rows)
        key_depth = lax.dynamic_slice_in_dim(depth_whole, key_start, block_rows)
        key_end = lax.dynamic_slice_in_dim(end_whole, key_start, block_rows)
        query_file = lax.dynamic_slice_in_dim(file_whole, query_start, block_rows)
        key_file = lax.dynamic_slice_in_dim(file_whole, key_start, block_rows)
        query_pos = query_start + jnp.arange(block_rows, dtype=jnp.int32)
        key_pos = key_start + jnp.arange(block_rows, dtype=jnp.int32)
        earlier = key_pos[None, :] <= query_pos[:, None]
        distance = jnp.abs(query_depth[:, None] - key_depth[None, :]).astype(jnp.float32)
        ancestor = (earlier & (query_pos[:, None] < key_end[None, :])).astype(jnp.float32)
        allowed = earlier & (query_file[:, None] == key_file[None, :])
        scores = (
            raw
            - local_slopes[:, None, None] * distance[None]
            + local_gains[:, None, None] * ancestor[None]
        )
        scores = jnp.where(allowed[None], scores, masked_score)
        return (scores, distance, ancestor)

    query_blocks = []
    key_acc = jnp.zeros((seq_len, HEAD_WIDTH), jnp.float32)
    value_acc = jnp.zeros((seq_len, HEAD_WIDTH), jnp.float32)
    slope_acc = jnp.zeros((local_heads,), jnp.float32)
    gain_acc = jnp.zeros((local_heads,), jnp.float32)
    for block_index in range(num_blocks):
        query_start = block_index * block_rows
        query_block = query_heads[query_start : query_start + block_rows]
        grad_block = grad_heads[query_start : query_start + block_rows]
        delta_block = row_delta[query_start : query_start + block_rows].T

        def statistics(key_block_index, running):
            row_top, row_total = running
            key_start = key_block_index * block_rows
            key_block = lax.dynamic_slice_in_dim(key_head, key_start, block_rows, 0)
            scores, _, _ = tile_block(query_block, key_block, query_start, key_start)
            new_top = jnp.maximum(row_top, jnp.max(scores, axis=2))
            row_total = row_total * jnp.exp(row_top - new_top) + jnp.sum(
                jnp.exp(scores - new_top[:, :, None]), axis=2
            )
            return (new_top, row_total)

        start_top = jnp.full((local_heads, block_rows), masked_score, jnp.float32)
        start_total = jnp.zeros((local_heads, block_rows), jnp.float32)
        row_top, row_total = lax.fori_loop(0, block_index + 1, statistics, (start_top, start_total))
        log_total = row_top + jnp.log(row_total)

        def gradients(key_block_index, running):
            query_acc, key_sums, value_sums, slope_sums, gain_sums = running
            key_start = key_block_index * block_rows
            key_block = lax.dynamic_slice_in_dim(key_head, key_start, block_rows, 0)
            value_block = lax.dynamic_slice_in_dim(value_head, key_start, block_rows, 0)
            scores, distance, ancestor = tile_block(query_block, key_block, query_start, key_start)
            probs = jnp.exp(scores - log_total[:, :, None])
            probs_b = probs.astype(jnp.bfloat16)
            dprobs = jnp.einsum(
                "qhe,ke->hqk", grad_block, value_block, preferred_element_type=jnp.float32
            )
            dscores = probs * (dprobs - delta_block[:, :, None])
            dscores_b = dscores.astype(jnp.bfloat16)
            query_acc = query_acc + jnp.einsum(
                "hqk,ke->qhe", dscores_b, key_block, preferred_element_type=jnp.float32
            )
            key_part = jnp.einsum(
                "hqk,qhe->ke", dscores_b, query_block, preferred_element_type=jnp.float32
            )
            value_part = jnp.einsum(
                "hqk,qhe->ke", probs_b, grad_block, preferred_element_type=jnp.float32
            )
            key_sums = add_rows(key_sums, key_part, key_start)
            value_sums = add_rows(value_sums, value_part, key_start)
            slope_sums = slope_sums - jnp.sum(dscores * distance[None], axis=(1, 2))
            gain_sums = gain_sums + jnp.sum(dscores * ancestor[None], axis=(1, 2))
            return (query_acc, key_sums, value_sums, slope_sums, gain_sums)

        query_start_acc = jnp.zeros((block_rows, local_heads, HEAD_WIDTH), jnp.float32)
        query_acc, key_acc, value_acc, slope_acc, gain_acc = lax.fori_loop(
            0,
            block_index + 1,
            gradients,
            (query_start_acc, key_acc, value_acc, slope_acc, gain_acc),
        )
        query_blocks.append(query_acc)
    query_grad = (jnp.concatenate(query_blocks, axis=0) * factor).astype(jnp.bfloat16)
    query_grad = query_grad.reshape(seq_len, 1, local_heads * HEAD_WIDTH)
    query_back = lax.all_to_all(query_grad, "ctx", split_axis=0, concat_axis=1, tiled=True)
    query_grads = query_back.reshape(1, tokens_here, heads_all * HEAD_WIDTH)
    key_scaled = (key_acc * factor).reshape(seq_len, 1, HEAD_WIDTH)
    value_scaled = value_acc.reshape(seq_len, 1, HEAD_WIDTH)
    key_back, value_back = (
        lax.all_to_all(
            key_scaled.astype(jnp.bfloat16), "ctx", split_axis=0, concat_axis=1, tiled=True
        ).astype(key_scaled.dtype),
        lax.all_to_all(
            value_scaled.astype(jnp.bfloat16), "ctx", split_axis=0, concat_axis=1, tiled=True
        ).astype(value_scaled.dtype),
    )
    key_grads = jnp.sum(key_back.reshape(tokens_here, kv_heads, repeats, HEAD_WIDTH), axis=2)
    value_grads = jnp.sum(value_back.reshape(tokens_here, kv_heads, repeats, HEAD_WIDTH), axis=2)
    key_grads = key_grads.astype(jnp.bfloat16).reshape(1, tokens_here, kv_heads * HEAD_WIDTH)
    value_grads = value_grads.astype(jnp.bfloat16).reshape(1, tokens_here, kv_heads * HEAD_WIDTH)
    bias_local = jnp.stack([slope_acc, gain_acc], axis=1)
    bias_grads = lax.psum(bias_local, "dp")
    return (query_grads, key_grads, value_grads, bias_grads)


def solution(mesh):
    in_specs = (
        P("dp", "ctx", None),
        P("dp", "ctx", None),
        P("dp", "ctx", None),
        P("dp", "ctx", None),
        P("dp", "ctx", None),
        P("dp", "ctx"),
        P("dp", "ctx"),
        P("dp", None),
        P(),
        P(),
    )
    out_specs = (P("dp", "ctx", None), P("dp", "ctx", None), P("dp", "ctx", None), P("ctx", None))
    return jax.shard_map(body, mesh=mesh, in_specs=in_specs, out_specs=out_specs, check_vma=False)
```

profile of v0, /device:TPU:6, one launch (start us, length us, event | category | flops | bytes accessed | tf_op | source)
XLA Modules:
  0.0 816.9 jit_solution(6041497727922549176)
XLA Ops:
  10.7 10.1 %all-to-all-start = ((bf16[128,16,256]{2,0,1:T(8,128)(2,1)}), bf16[128,16,256]{2,0,1:T(8,128)(2,1)S(1)}, u32[]{:S(2)}, u32[]{:S(2)}) async-start(bf16[128,16,256]{2,0,1:T(8,128)(2,1)} %copy.270), calls=%async_computation | async-start | bytes 2097152 | tf_op jit(solution)/shard_map/all_to_all | solution.py:61
  23.6 28.2 %all-to-all-done = bf16[128,16,256]{2,0,1:T(8,128)(2,1)S(1)} async-done(((bf16[128,16,256]{2,0,1:T(8,128)(2,1)}), bf16[128,16,256]{2,0,1:T(8,128)(2,1)S(1)}, u32[]{:S(2)}, u32[]{:S(2)}) %all-to-all-start) | async-done | bytes 1048608 | tf_op jit(solution)/shard_map/all_to_all | solution.py:61
  61.8 29.8 %all-to-all-done.1 = bf16[128,16,256]{2,0,1:T(8,128)(2,1)S(1)} async-done(((bf16[128,16,256]{2,0,1:T(8,128)(2,1)}), bf16[128,16,256]{2,0,1:T(8,128)(2,1)S(1)}, u32[]{:S(2)}, u32[]{:S(2)}) %all-to-all-start.1) | async-done | bytes 1048608 | tf_op jit(solution)/shard_map/all_to_all | solution.py:62
  91.6 8.7 %all-to-all-start.2 = ((bf16[128,16,256]{2,0,1:T(8,128)(2,1)}), bf16[128,16,256]{2,0,1:T(8,128)(2,1)}, u32[]{:S(2)}, u32[]{:S(2)}) async-start(bf16[128,16,256]{2,0,1:T(8,128)(2,1)} %copy.274), calls=%async_computation.2 | async-start | bytes 2097152 | tf_op jit(solution)/shard_map/all_to_all | solution.py:63
  101.0 50.5 %all_gather.13 = s32[1,2048]{1,0:T(1,128)S(1)} all-gather(s32[1,128]{1,0:T(1,128)S(1)} %copy-done.46), channel_id=1, replica_groups=mesh['dp'=32,'ctx'=16] {'ctx'}, dimensions={1}, use_global_device_ids=true | all-gather | bytes 8704 | tf_op jit(solution)/shard_map/all_gather | solution.py:50
  151.5 40.5 %all_gather.14 = s32[1,2048]{1,0:T(1,128)} all-gather(s32[1,128]{1,0:T(1,128)S(1)} %copy-done.47), channel_id=1, replica_groups=mesh['dp'=32,'ctx'=16] {'ctx'}, dimensions={1}, use_global_device_ids=true | all-gather | bytes 8704 | tf_op jit(solution)/shard_map/all_gather | solution.py:51
  225.1 10.2 %while.281 = (s32[]{:T(128)}, f32[2,256]{1,0:T(2,128)}, f32[2,256]{1,0:T(2,128)}, s32[2048]{0:T(1024)S(1)}, bf16[2048,128]{1,0:T(8,128)(2,1)S(1)}, /*index=5*/bf...) while((s32[]{:T(128)}, f32[2,256]{1,0:T(2,128)}, ...), condition=%wide.region_10.11_spmd.clone, body=%wide.region_7.10_spmd.clone.sunk | while | flops 35326980 | bytes 2471134 | solution.py:124
  238.4 16.9 %while.282 = (s32[]{:T(128)}, f32[256,2,128]{0,2,1:T(8,128)}, f32[2048,128]{1,0:T(8,128)S(1)}, f32[2048,128]{1,0:T(8,128)S(1)}, f32[2]{0:T(128)}, /*index=5*/f32...) while((s32[]{:T(128)}, f32[256,2,128]{0,2,1:T(8,128)}, ...), condition=%wide.region_14.15_spmd.clone, body=%wide.region_11.14_spmd.clone.sunk | while | flops 170525184 | bytes 6905245 | solution.py:156
  255.3 15.9 %while.283 = (s32[]{:T(128)}, f32[2,256]{1,0:T(2,128)}, f32[2,256]{1,0:T(2,128)}, s32[2048]{0:T(1024)S(1)}, bf16[2048,128]{1,0:T(8,128)(2,1)S(1)}, /*index=5*/bf...) while((s32[]{:T(128)}, f32[2,256]{1,0:T(2,128)}, ...), condition=%wide.region_18.19_spmd.clone, body=%wide.region_15.18_spmd.clone.sunk | while | flops 35326980 | bytes 2471134 | solution.py:124
  272.4 26.0 %while.284 = (s32[]{:T(128)}, f32[256,2,128]{0,2,1:T(8,128)}, f32[2048,128]{1,0:T(8,128)S(1)}, f32[2048,128]{1,0:T(8,128)S(1)}, f32[2]{0:T(128)}, /*index=5*/f32...) while((s32[]{:T(128)}, f32[256,2,128]{0,2,1:T(8,128)}, ...), condition=%wide.region_22.23_spmd.clone, body=%wide.region_19.22_spmd.clone.sunk | while | flops 170525184 | bytes 6905245 | solution.py:156
  298.4 21.7 %while.285 = (s32[]{:T(128)}, f32[2,256]{1,0:T(2,128)}, f32[2,256]{1,0:T(2,128)}, s32[2048]{0:T(1024)S(1)}, bf16[2048,128]{1,0:T(8,128)(2,1)S(1)}, /*index=5*/bf...) while((s32[]{:T(128)}, f32[2,256]{1,0:T(2,128)}, ...), condition=%wide.region_26.27_spmd.clone, body=%wide.region_23.26_spmd.clone.sunk | while | flops 35326980 | bytes 2471134 | solution.py:124
  321.4 35.1 %while.286 = (s32[]{:T(128)}, f32[256,2,128]{0,2,1:T(8,128)}, f32[2048,128]{1,0:T(8,128)S(1)}, f32[2048,128]{1,0:T(8,128)S(1)}, f32[2]{0:T(128)}, /*index=5*/f32...) while((s32[]{:T(128)}, f32[256,2,128]{0,2,1:T(8,128)}, ...), condition=%wide.region_30.31_spmd.clone, body=%wide.region_27.30_spmd.clone.sunk | while | flops 170525184 | bytes 6905245 | solution.py:156
  356.5 27.0 %while.287 = (s32[]{:T(128)}, f32[2,256]{1,0:T(2,128)}, f32[2,256]{1,0:T(2,128)}, s32[2048]{0:T(1024)S(1)}, bf16[2048,128]{1,0:T(8,128)(2,1)S(1)}, /*index=5*/bf...) while((s32[]{:T(128)}, f32[2,256]{1,0:T(2,128)}, ...), condition=%wide.region_34.35_spmd.clone, body=%wide.region_31.34_spmd.clone.sunk | while | flops 35326980 | bytes 2471134 | solution.py:124
  384.8 43.8 %while.288 = (s32[]{:T(128)}, f32[256,2,128]{0,2,1:T(8,128)}, f32[2048,128]{1,0:T(8,128)S(1)}, f32[2048,128]{1,0:T(8,128)S(1)}, f32[2]{0:T(128)}, /*index=5*/f32...) while((s32[]{:T(128)}, f32[256,2,128]{0,2,1:T(8,128)}, ...), condition=%wide.region_38.39_spmd.clone, body=%wide.region_35.38_spmd.clone.sunk | while | flops 170525184 | bytes 6905245 | solution.py:156
  428.6 31.9 %while.289 = (s32[]{:T(128)}, f32[2,256]{1,0:T(2,128)}, f32[2,256]{1,0:T(2,128)}, s32[2048]{0:T(1024)S(1)}, bf16[2048,128]{1,0:T(8,128)(2,1)S(1)}, /*index=5*/bf...) while((s32[]{:T(128)}, f32[2,256]{1,0:T(2,128)}, ...), condition=%wide.region_42.43_spmd.clone, body=%wide.region_39.42_spmd.clone.sunk | while | flops 35326980 | bytes 2471134 | solution.py:124
  461.7 52.9 %while.290 = (s32[]{:T(128)}, f32[256,2,128]{0,2,1:T(8,128)}, f32[2048,128]{1,0:T(8,128)S(1)}, f32[2048,128]{1,0:T(8,128)S(1)}, f32[2]{0:T(128)}, /*index=5*/f32...) while((s32[]{:T(128)}, f32[256,2,128]{0,2,1:T(8,128)}, ...), condition=%wide.region_46.47_spmd.clone, body=%wide.region_43.46_spmd.clone.sunk | while | flops 170525184 | bytes 6380929 | solution.py:156
  514.6 35.6 %while.291 = (s32[]{:T(128)}, f32[2,256]{1,0:T(2,128)}, f32[2,256]{1,0:T(2,128)}, s32[2048]{0:T(1024)S(1)}, bf16[2048,128]{1,0:T(8,128)(2,1)S(1)}, /*index=5*/bf...) while((s32[]{:T(128)}, f32[2,256]{1,0:T(2,128)}, ...), condition=%wide.region_50.51_spmd.clone, body=%wide.region_47.50_spmd.clone.sunk | while | flops 35326980 | bytes 2471134 | solution.py:124
  550.9 44.9 %while.292 = (s32[]{:T(128)}, f32[256,2,128]{0,2,1:T(8,128)}, f32[2048,128]{1,0:T(8,128)S(1)}, f32[2048,128]{1,0:T(8,128)S(1)}, f32[2]{0:T(128)}, /*index=5*/f32...) while((s32[]{:T(128)}, f32[256,2,128]{0,2,1:T(8,128)}, ...), condition=%wide.region_54.55_spmd.clone, body=%wide.region_51.54_spmd.clone.sunk | while | flops 170525184 | bytes 6381169 | solution.py:156
  595.8 27.2 %while.293 = (s32[]{:T(128)}, f32[2,256]{1,0:T(2,128)}, f32[2,256]{1,0:T(2,128)}, s32[2048]{0:T(1024)S(1)}, bf16[2048,128]{1,0:T(8,128)(2,1)S(1)}, /*index=5*/bf...) while((s32[]{:T(128)}, f32[2,256]{1,0:T(2,128)}, ...), condition=%wide.region_58.59_spmd.clone, body=%wide.region_55.58_spmd.clone.sunk | while | flops 35326980 | bytes 2495794 | solution.py:124
  623.7 38.1 %while.294 = (s32[]{:T(128)}, f32[256,2,128]{0,2,1:T(8,128)}, f32[2048,128]{1,0:T(8,128)S(1)}, f32[2048,128]{1,0:T(8,128)S(1)}, f32[2]{0:T(128)S(1)}, /*index=5*...) while((s32[]{:T(128)}, f32[256,2,128]{0,2,1:T(8,128)}, ...), condition=%wide.region_62.63_spmd.clone, body=%wide.region_59.62_spmd.clone.sunk | while | flops 170525184 | bytes 7953821 | solution.py:156
  664.5 13.1 %all-to-all-start.5 = ((bf16[16,2,8192]{2,1,0:T(2,128)(2,1)}), bf16[16,2,8192]{2,1,0:T(2,128)(2,1)S(1)}, u32[]{:S(2)}, u32[]{:S(2)}) async-start(bf16[16,2,8192]{2,1,0:T(2,128)(2,1)} %reshape.2664), calls=%async_computation.5 | async-start | bytes 1048576 | tf_op jit(solution)/shard_map/all_to_all | solution.py:173
  704.3 11.6 %reduce.2 = bf16[2048,256]{1,0:T(8,128)(2,1)} reduce(bf16[2048,1,256]{2,1,0:T(2,128)(2,1)S(1)} %multiply_convert_fusion, bf16[]{:T(256)} %broadcast.2310), dimensions={1}, to_apply=%multiply_convert_fusion.reduce_sub_computation | reduce | bytes 2097154 | tf_op jit(solution)/shard_map/convert_element_type | solution.py:163
  718.1 9.6 %all-to-all-start.3 = ((bf16[16,2,16384]{2,1,0:T(2,128)(2,1)}), bf16[16,2,16384]{2,1,0:T(2,128)(2,1)}, u32[]{:S(2)}, u32[]{:S(2)}) async-start(bf16[16,2,16384]{2,1,0:T(2,128)(2,1)} %reshape.2660), calls=%async_computation.3 | async-start | bytes 2097152 | tf_op jit(solution)/shard_map/all_to_all | solution.py:165
  727.7 70.1 %psum.7 = f32[2,2]{0,1:T(2,128)S(1)} all-reduce(f32[2,2]{0,1:T(2,128)S(1)} %pad_maximum_fusion), channel_id=1, replica_groups=mesh['dp'=32,'ctx'=16] {'dp'}, use_global_device_ids=true, to_apply=%region_65.66 | all-reduce | flops 4 | bytes 32 | tf_op jit(solution)/shard_map/psum | solution.py:182
  (1215 shorter events, 526.3 us)
Async XLA Ops:
  7.2 212.6 %all-gather.5.cloned.1.call-start = ((), (), s32[]{:S(2)}) async-start(), calls=%async_computation.6 | async-start | bytes 2228224 | tf_op jit(solution)/shard_map/all_gather | solution.py:70
  10.7 41.1 %all-to-all-start = ((bf16[128,16,256]{2,0,1:T(8,128)(2,1)}), bf16[128,16,256]{2,0,1:T(8,128)(2,1)S(1)}, u32[]{:S(2)}, u32[]{:S(2)}) async-start(bf16[128,16,256]{2,0,1:T(8,128)(2,1)} %copy.270), calls=%async_computation | async-start | bytes 2097152 | tf_op jit(solution)/shard_map/all_to_all | solution.py:61
  51.8 39.8 %all-to-all-start.1 = ((bf16[128,16,256]{2,0,1:T(8,128)(2,1)}), bf16[128,16,256]{2,0,1:T(8,128)(2,1)S(1)}, u32[]{:S(2)}, u32[]{:S(2)}) async-start(bf16[128,16,256]{2,0,1:T(8,128)(2,1)} %copy.272), calls=%async_computation.1 | async-start | bytes 2097152 | tf_op jit(solution)/shard_map/all_to_all | solution.py:62
  58.2 163.2 %all-gather.7.cloned.1.call-start = ((), (), s32[]{:S(2)}) async-start(), calls=%async_computation.7 | async-start | bytes 2228224 | tf_op jit(solution)/shard_map/all_gather | solution.py:71
  60.4 40.1 %copy-start.53 = (f32[32]{0:T(128)S(1)}, f32[32]{0:T(128)}, u32[]{:S(2)}) copy-start(f32[32]{0:T(128)} %param.46) | copy-start | bytes 388
  60.4 40.2 %copy-start.54 = (f32[32]{0:T(128)S(1)}, f32[32]{0:T(128)}, u32[]{:S(2)}) copy-start(f32[32]{0:T(128)} %param.47) | copy-start | bytes 388
  60.4 40.3 %copy-start.55 = (s32[1,8]{1,0:T(1,128)S(1)}, s32[1,8]{1,0:T(1,128)}, u32[]{:S(2)}) copy-start(s32[1,8]{1,0:T(1,128)} %param.45) | copy-start | bytes 100
  60.4 40.6 %copy-start.46 = (s32[1,128]{1,0:T(1,128)S(1)}, s32[1,128]{1,0:T(1,128)}, u32[]{:S(2)}) copy-start(s32[1,128]{1,0:T(1,128)} %param.43) | copy-start | bytes 1540
  60.4 91.1 %copy-start.47 = (s32[1,128]{1,0:T(1,128)S(1)}, s32[1,128]{1,0:T(1,128)}, u32[]{:S(2)}) copy-start(s32[1,128]{1,0:T(1,128)} %param.44) | copy-start | bytes 1540
  91.6 103.8 %all-to-all-start.2 = ((bf16[128,16,256]{2,0,1:T(8,128)(2,1)}), bf16[128,16,256]{2,0,1:T(8,128)(2,1)}, u32[]{:S(2)}, u32[]{:S(2)}) async-start(bf16[128,16,256]{2,0,1:T(8,128)(2,1)} %copy.274), calls=%async_computation.2 | async-start | bytes 2097152 | tf_op jit(solution)/shard_map/all_to_all | solution.py:63
  100.6 119.1 %copy-start.23 = (f32[2]{0:T(128)}, f32[2]{0:T(128)S(1)}, u32[]{:S(2)}) copy-start(f32[2]{0:T(128)S(1)} %dynamic_slice.792) | copy-start | bytes 28
  100.7 119.1 %copy-start.24 = (f32[2]{0:T(128)}, f32[2]{0:T(128)S(1)}, u32[]{:S(2)}) copy-start(f32[2]{0:T(128)S(1)} %dynamic_slice.794) | copy-start | bytes 28
  461.7 52.9 %copy-start.5 = (bf16[256,2,128]{2,0,1:T(8,128)(2,1)S(1)}, bf16[256,2,128]{2,0,1:T(8,128)(2,1)}, u32[]{:S(2)}) copy-start(bf16[256,2,128]{2,0,1:T(8,128)(2,1)} %copy.301) | copy-start | bytes 393220
  550.9 44.9 %copy-start.4 = (bf16[256,2,128]{2,0,1:T(8,128)(2,1)S(1)}, bf16[256,2,128]{2,0,1:T(8,128)(2,1)}, u32[]{:S(2)}) copy-start(bf16[256,2,128]{2,0,1:T(8,128)(2,1)} %copy.305) | copy-start | bytes 393220
  595.8 27.9 %copy-start.37 = (f32[256,2]{0,1:T(2,128)S(1)}, f32[256,2]{0,1:T(2,128)}, u32[]{:S(2)}) copy-start(f32[256,2]{0,1:T(2,128)} %copy.354) | copy-start | bytes 6148
  595.8 27.9 %copy-start.43 = (f32[2]{0:T(128)S(1)}, f32[2]{0:T(128)}, u32[]{:S(2)}) copy-start(f32[2]{0:T(128)} %get-tuple-element.7581) | copy-start | bytes 28
  595.8 27.9 %copy-start.50 = (f32[2]{0:T(128)S(1)}, f32[2]{0:T(128)}, u32[]{:S(2)}) copy-start(f32[2]{0:T(128)} %get-tuple-element.7580) | copy-start | bytes 28
  663.6 16.0 %copy-start.17 = (f32[256,2,128]{0,2,1:T(8,128)S(1)}, f32[256,2,128]{0,2,1:T(8,128)}, u32[]{:S(2)}) copy-start(f32[256,2,128]{0,2,1:T(8,128)} %get-tuple-element.3250) | copy-start | bytes 786436
  664.5 15.4 %copy-start.19 = (f32[256,2,128]{0,2,1:T(8,128)S(1)}, f32[256,2,128]{0,2,1:T(8,128)}, u32[]{:S(2)}) copy-start(f32[256,2,128]{0,2,1:T(8,128)} %get-tuple-element.3236) | copy-start | bytes 786436
  664.5 24.2 %all-to-all-start.5 = ((bf16[16,2,8192]{2,1,0:T(2,128)(2,1)}), bf16[16,2,8192]{2,1,0:T(2,128)(2,1)S(1)}, u32[]{:S(2)}, u32[]{:S(2)}) async-start(bf16[16,2,8192]{2,1,0:T(2,128)(2,1)} %reshape.2664), calls=%async_computation.5 | async-start | bytes 1048576 | tf_op jit(solution)/shard_map/all_to_all | solution.py:173
  681.3 16.1 %copy-start.14 = (f32[256,2,128]{0,2,1:T(8,128)S(1)}, f32[256,2,128]{0,2,1:T(8,128)}, u32[]{:S(2)}) copy-start(f32[256,2,128]{0,2,1:T(8,128)} %get-tuple-element.3271) | copy-start | bytes 786436
  681.5 16.1 %copy-start.15 = (f32[256,2,128]{0,2,1:T(8,128)S(1)}, f32[256,2,128]{0,2,1:T(8,128)}, u32[]{:S(2)}) copy-start(f32[256,2,128]{0,2,1:T(8,128)} %get-tuple-element.3264) | copy-start | bytes 786436
  688.7 29.3 %all-to-all-start.4 = ((bf16[16,2,8192]{2,1,0:T(2,128)(2,1)}), bf16[16,2,8192]{2,1,0:T(2,128)(2,1)S(1)}, u32[]{:S(2)}, u32[]{:S(2)}) async-start(bf16[16,2,8192]{2,1,0:T(2,128)(2,1)} %reshape.2662), calls=%async_computation.4 | async-start | bytes 1048576 | tf_op jit(solution)/shard_map/all_to_all | solution.py:170
  718.1 83.6 %all-to-all-start.3 = ((bf16[16,2,16384]{2,1,0:T(2,128)(2,1)}), bf16[16,2,16384]{2,1,0:T(2,128)(2,1)}, u32[]{:S(2)}, u32[]{:S(2)}) async-start(bf16[16,2,16384]{2,1,0:T(2,128)(2,1)} %reshape.2660), calls=%async_computation.3 | async-start | bytes 2097152 | tf_op jit(solution)/shard_map/all_to_all | solution.py:165
  (130 other events, 403.9 us)
Sparse Core Ops, SparseCore 0:
  11.0 90.2 all-gather.4
  104.3 77.3 all-gather.6
where the time goes:
time: 825 us; the launch traced here: 817 us
  matrix products  215 us (26%)
  blocking collectives  161 us (20%)
  other arithmetic  160 us (19%)
  local copies, waits for them, and re-layouts  144 us (17%)
  waiting for transfers between devices  63.2 us (8%)
  starting transfers between devices  55.7 us (7%)
  between operations  14.9 us (2%)
    dot_general x71, matrix products, tile_block(): jnp.einsum('qhe,ke->hqk', query_block, key_block, preferred_element_type=...  95.1 us
    psum x1, blocking collectives, body(): bias_grads = lax.psum(bias_local, 'dp')  70.1 us
    dot_general x36, matrix products, gradients(): jnp.einsum('qhe,ke->hqk', grad_block, value_block, preferred_element_type...  56 us
    dynamic_slice x71, local copies, waits for them, and re-layouts, tile_block(): key_end = lax.dynamic_slice_in_dim(end_whole, key_start, block_rows)  53.7 us
    all_gather x1, blocking collectives, body(): lax.all_gather(depths, 'ctx', axis=1, tiled=True)  50.5 us
    dot_general x36, matrix products, gradients(): jnp.einsum('hqk,ke->qhe', dscores_b, key_block, preferred_element_type=jn...  48.5 us
    all_gather x1, blocking collectives, body(): lax.all_gather(subtree_end, 'ctx', axis=1, tiled=True)  40.5 us
    unnamed x119, local copies, waits for them, and re-layouts  37.6 us
  transfers between devices with their start and end apart: 8, of which 3 were waited for; matrix products, arithmetic and copies ran while one was open for 9% of the time, Pallas kernels for 0%

commit v1 on v0

v1 whole, which is shorter than its diff:
```python
import functools

import jax
import jax.numpy as jnp
from jax import lax
from jax.experimental import pallas as pl
from jax.experimental.pallas import tpu as pltpu
from jax.sharding import PartitionSpec as P

HEAD_WIDTH = 128
BLOCK = 256

masked_score = -1e30


def _grads_kernel(
    lo_ref,
    sg_ref,
    q_ref,
    qT_ref,
    do_ref,
    doT_ref,
    delta_ref,
    k_ref,
    kT_ref,
    vT_ref,
    dcol_ref,
    fcol_ref,
    drow_ref,
    frow_ref,
    erow_ref,
    dq_ref,
    dkT_ref,
    dvT_ref,
    bias_ref,
    s_scr,
    m_scr,
    l_scr,
    dq_scr,
    *,
    nh,
    hw,
    bq,
    bk,
    factor,
):
    i = pl.program_id(0)

    @pl.when(i == 0)
    def _():
        dkT_ref[...] = jnp.zeros_like(dkT_ref)
        dvT_ref[...] = jnp.zeros_like(dvT_ref)
        bias_ref[...] = jnp.zeros_like(bias_ref)

    q0 = i * bq
    lo = lo_ref[i]
    qpos = q0 + lax.broadcasted_iota(jnp.int32, (bq, 1), 0)
    dcol = dcol_ref[...]
    fcol = fcol_ref[...]

    def tile_masks(kb):
        k0 = pl.multiple_of(kb * bk, bk)
        kpos = k0 + lax.broadcasted_iota(jnp.int32, (1, bk), 1)
        drow = drow_ref[:, pl.ds(k0, bk)]
        frow = frow_ref[:, pl.ds(k0, bk)]
        erow = erow_ref[:, pl.ds(k0, bk)]
        causal = kpos <= qpos
        allowed = causal & (fcol == frow)
        anc = jnp.where(causal & (qpos < erow), 1.0, 0.0).astype(jnp.float32)
        dist = jnp.abs(dcol - drow).astype(jnp.float32)
        return k0, allowed, anc, dist

    m_scr[...] = jnp.full(m_scr.shape, masked_score, jnp.float32)
    l_scr[...] = jnp.zeros(l_scr.shape, jnp.float32)

    def stats(kb, carry):
        k0, allowed, anc, dist = tile_masks(kb)
        kT = kT_ref[:, pl.ds(k0, bk)]
        for h in range(nh):
            raw = jnp.dot(q_ref[:, h * hw : (h + 1) * hw], kT, preferred_element_type=jnp.float32)
            s = raw * factor
            s = s - sg_ref[h] * dist + sg_ref[nh + h] * anc
            s = jnp.where(allowed, s, masked_score)
            s_scr[h, kb] = s
            m_old = m_scr[h]
            m_new = jnp.maximum(m_old, jnp.max(s, axis=1, keepdims=True))
            l_scr[h] = l_scr[h] * jnp.exp(m_old - m_new) + jnp.sum(
                jnp.exp(s - m_new), axis=1, keepdims=True
            )
            m_scr[h] = m_new
        return carry

    lax.fori_loop(lo, i + 1, stats, 0)
    for h in range(nh):
        m_scr[h] = m_scr[h] + jnp.log(l_scr[h])
    dq_scr[...] = jnp.zeros(dq_scr.shape, jnp.float32)

    def grads(kb, carry):
        k0, _, anc, dist = tile_masks(kb)
        vT = vT_ref[:, pl.ds(k0, bk)]
        kblk = k_ref[pl.ds(k0, bk), :]
        for h in range(nh):
            s = s_scr[h, kb]
            p = jnp.exp(s - m_scr[h])
            dp = jnp.dot(do_ref[:, h * hw : (h + 1) * hw], vT, preferred_element_type=jnp.float32)
            ds = p * (dp - delta_ref[:, h : h + 1])
            ds_b = ds.astype(jnp.bfloat16)
            p_b = p.astype(jnp.bfloat16)
            dq_scr[h] += jnp.dot(ds_b, kblk, preferred_element_type=jnp.float32)
            dkT_ref[:, pl.ds(k0, bk)] += jnp.dot(
                qT_ref[h * hw : (h + 1) * hw, :], ds_b, preferred_element_type=jnp.float32
            )
            dvT_ref[:, pl.ds(k0, bk)] += jnp.dot(
                doT_ref[h * hw : (h + 1) * hw, :], p_b, preferred_element_type=jnp.float32
            )
            bias_ref[h] += jnp.sum(ds * dist, axis=0, keepdims=True)
            bias_ref[nh + h] += jnp.sum(ds * anc, axis=0, keepdims=True)
        return carry

    lax.fori_loop(lo, i + 1, grads, 0)
    for h in range(nh):
        dq_ref[:, h * hw : (h + 1) * hw] = (dq_scr[h] * factor).astype(dq_ref.dtype)


def attention_grads(q, qT, do, doT, delta, k, kT, vT, dcol, fcol, drow, frow, erow, lo, sg, interpret=False):
    seq_len, width = q.shape
    hw = k.shape[1]
    nh = width // hw
    bq = bk = min(BLOCK, seq_len)
    nq = seq_len // bq
    nk = seq_len // bk
    factor = hw ** (-0.5)
    kernel = functools.partial(_grads_kernel, nh=nh, hw=hw, bq=bq, bk=bk, factor=factor)
    full = lambda shape: pl.BlockSpec(shape, lambda i, lo: (0,) * len(shape))
    grid_spec = pltpu.PrefetchScalarGridSpec(
        num_scalar_prefetch=1,
        grid=(nq,),
        in_specs=[
            pl.BlockSpec(memory_space=pltpu.SMEM),
            pl.BlockSpec((bq, width), lambda i, lo: (i, 0)),
            pl.BlockSpec((width, bq), lambda i, lo: (0, i)),
            pl.BlockSpec((bq, width), lambda i, lo: (i, 0)),
            pl.BlockSpec((width, bq), lambda i, lo: (0, i)),
            pl.BlockSpec((bq, nh), lambda i, lo: (i, 0)),
            full((seq_len, hw)),
            full((hw, seq_len)),
            full((hw, seq_len)),
            pl.BlockSpec((bq, 1), lambda i, lo: (i, 0)),
            pl.BlockSpec((bq, 1), lambda i, lo: (i, 0)),
            full((1, seq_len)),
            full((1, seq_len)),
            full((1, seq_len)),
        ],
        out_specs=[
            pl.BlockSpec((bq, width), lambda i, lo: (i, 0)),
            full((hw, seq_len)),
            full((hw, seq_len)),
            full((2 * nh, 1, bk)),
        ],
        scratch_shapes=[
            pltpu.VMEM((nh, nk, bq, bk), jnp.float32),
            pltpu.VMEM((nh, bq, 1), jnp.float32),
            pltpu.VMEM((nh, bq, 1), jnp.float32),
            pltpu.VMEM((nh, bq, hw), jnp.float32),
        ],
    )
    causal_tiles = nq * (nq + 1) // 2
    flops = 2 * 5 * nh * causal_tiles * bq * bk * hw
    return pl.pallas_call(
        kernel,
        grid_spec=grid_spec,
        out_shape=[
            jax.ShapeDtypeStruct((seq_len, width), jnp.bfloat16),
            jax.ShapeDtypeStruct((hw, seq_len), jnp.float32),
            jax.ShapeDtypeStruct((hw, seq_len), jnp.float32),
            jax.ShapeDtypeStruct((2 * nh, 1, bk), jnp.float32),
        ],
        compiler_params=pltpu.CompilerParams(
            dimension_semantics=("arbitrary",), vmem_limit_bytes=48 * 1024 * 1024
        ),
        cost_estimate=pl.CostEstimate(
            flops=flops,
            transcendentals=2 * nh * causal_tiles * bq * bk,
            bytes_accessed=8 * seq_len * width + 8 * seq_len * hw,
        ),
        interpret=interpret,
    )(lo, sg, q, qT, do, doT, delta, k, kT, vT, dcol, fcol, drow, frow, erow)


def body(
    queries,
    key_rows,
    values,
    outputs,
    out_grads,
    depths,
    subtree_end,
    file_lengths,
    slopes,
    ancestor_gain,
):
    tokens_here = queries.shape[1]
    context_size = lax.axis_size("ctx")
    heads_all = queries.shape[2] // HEAD_WIDTH
    kv_heads = key_rows.shape[2] // HEAD_WIDTH
    local_heads = heads_all // context_size
    group_width = heads_all // kv_heads
    repeats = context_size // kv_heads
    assert group_width // local_heads == repeats
    seq_len = tokens_here * context_size
    block = min(BLOCK, seq_len)
    factor = HEAD_WIDTH ** (-0.5)
    head_first = lax.axis_index("ctx") * local_heads
    local_slopes = lax.dynamic_slice_in_dim(slopes, head_first, local_heads)
    local_gains = lax.dynamic_slice_in_dim(ancestor_gain, head_first, local_heads)
    sg = jnp.concatenate([local_slopes, local_gains])
    depth_whole = lax.all_gather(depths[0], "ctx", axis=0, tiled=True)
    end_whole = lax.all_gather(subtree_end[0], "ctx", axis=0, tiled=True)
    positions = jnp.arange(seq_len, dtype=jnp.int32)
    lengths = file_lengths[0]
    bounds = jnp.cumsum(lengths)
    starts = bounds - lengths
    file_whole = jnp.sum((positions[:, None] >= bounds[None, :]).astype(jnp.int32), axis=1)
    file_start = starts[jnp.minimum(file_whole, lengths.shape[0] - 1)]
    lo = (file_start[::block] // block).astype(jnp.int32)

    delta_tok = jnp.sum(
        (out_grads[0].astype(jnp.float32) * outputs[0].astype(jnp.float32)).reshape(
            tokens_here, heads_all, HEAD_WIDTH
        ),
        axis=2,
    )
    delta_heads = lax.all_to_all(
        delta_tok.reshape(tokens_here, context_size, local_heads), "ctx", split_axis=1, concat_axis=0, tiled=True
    ).reshape(seq_len, local_heads)
    query_split = queries[0].reshape(tokens_here, context_size, local_heads * HEAD_WIDTH)
    grad_split = out_grads[0].reshape(tokens_here, context_size, local_heads * HEAD_WIDTH)
    query_heads = lax.all_to_all(query_split, "ctx", split_axis=1, concat_axis=0, tiled=True)
    grad_heads = lax.all_to_all(grad_split, "ctx", split_axis=1, concat_axis=0, tiled=True)
    query_heads = query_heads.reshape(seq_len, local_heads * HEAD_WIDTH)
    grad_heads = grad_heads.reshape(seq_len, local_heads * HEAD_WIDTH)
    key_rep = jnp.repeat(key_rows[0].reshape(tokens_here, kv_heads, HEAD_WIDTH), repeats, axis=1)
    value_rep = jnp.repeat(values[0].reshape(tokens_here, kv_heads, HEAD_WIDTH), repeats, axis=1)
    key_head = lax.all_to_all(key_rep, "ctx", split_axis=1, concat_axis=0, tiled=True).reshape(seq_len, HEAD_WIDTH)
    value_head = lax.all_to_all(value_rep, "ctx", split_axis=1, concat_axis=0, tiled=True).reshape(
        seq_len, HEAD_WIDTH
    )

    dq, dkT, dvT, bias_part = attention_grads(
        query_heads,
        query_heads.T,
        grad_heads,
        grad_heads.T,
        delta_heads,
        key_head,
        key_head.T,
        value_head.T,
        depth_whole[:, None],
        file_whole[:, None],
        depth_whole[None, :],
        file_whole[None, :],
        end_whole[None, :],
        lo,
        sg,
    )

    query_back = lax.all_to_all(
        dq.reshape(seq_len, 1, local_heads * HEAD_WIDTH), "ctx", split_axis=0, concat_axis=1, tiled=True
    )
    query_grads = query_back.reshape(1, tokens_here, heads_all * HEAD_WIDTH)
    key_scaled = (dkT.T * factor).reshape(seq_len, 1, HEAD_WIDTH)
    value_scaled = dvT.T.reshape(seq_len, 1, HEAD_WIDTH)
    key_back = lax.all_to_all(
        key_scaled.astype(jnp.bfloat16), "ctx", split_axis=0, concat_axis=1, tiled=True
    ).astype(jnp.float32)
    value_back = lax.all_to_all(
        value_scaled.astype(jnp.bfloat16), "ctx", split_axis=0, concat_axis=1, tiled=True
    ).astype(jnp.float32)
    key_grads = jnp.sum(key_back.reshape(tokens_here, kv_heads, repeats, HEAD_WIDTH), axis=2)
    value_grads = jnp.sum(value_back.reshape(tokens_here, kv_heads, repeats, HEAD_WIDTH), axis=2)
    key_grads = key_grads.astype(jnp.bfloat16).reshape(1, tokens_here, kv_heads * HEAD_WIDTH)
    value_grads = value_grads.astype(jnp.bfloat16).reshape(1, tokens_here, kv_heads * HEAD_WIDTH)
    bias_sums = jnp.sum(bias_part, axis=(1, 2))
    bias_local = jnp.stack([-bias_sums[:local_heads], bias_sums[local_heads:]], axis=1)
    bias_grads = lax.psum(bias_local, "dp")
    return (query_grads, key_grads, value_grads, bias_grads)


def solution(mesh):
    in_specs = (
        P("dp", "ctx", None),
        P("dp", "ctx", None),
        P("dp", "ctx", None),
        P("dp", "ctx", None),
        P("dp", "ctx", None),
        P("dp", "ctx"),
        P("dp", "ctx"),
        P("dp", None),
        P(),
        P(),
    )
    out_specs = (P("dp", "ctx", None), P("dp", "ctx", None), P("dp", "ctx", None), P("ctx", None))
    return jax.shard_map(body, mesh=mesh, in_specs=in_specs, out_specs=out_specs, check_vma=False)
```

time: 825 us -> 367 us (0.44)
  matrix products: 215 us -> 0 us
  other arithmetic: 160 us -> 11.8 us
  local copies, waits for them, and re-layouts: 144 us -> 32.3 us
  Pallas kernels: 0 us -> 37.6 us
  blocking collectives: 161 us -> 141 us
  waiting for transfers between devices: 63.2 us -> 79.8 us
  between operations: 14.9 us -> 0.97 us
    dot_general x215 -> x0, matrix products: 215 us -> none  [the longest x71 95.1 us: tile_block(): jnp.einsum('qhe,ke->hqk', query_block, key_block, preferred_element_type=...]
    dynamic_slice x145 -> x0, local copies, waits for them, and re-layouts: 62 us -> none  [the longest x71 53.7 us: tile_block(): key_end = lax.dynamic_slice_in_dim(end_whole, key_start, block_rows)]
    add x148 -> x0, other arithmetic: 61.7 us -> none  [the longest x35 30.2 us: statistics(): row_total * jnp.exp(row_top - new_top)]
    pallas_call x0 -> x1, Pallas kernels: none -> 37.6 us  [attention_grads(): pl.pallas_call(kernel, grid_spec=grid_spec, out_shape=[jax.ShapeDtypeStru...]
    all_to_all x2 -> x4, waiting for transfers between devices: 0.01 us -> 35.1 us  [the longest x1 15 us: body(): lax.all_to_all(key_rep, 'ctx', split_axis=1, concat_axis=0, tiled=True)]
    while x260 -> x0, local copies, waits for them, and re-layouts: 30.6 us -> none
    all_to_all x1, waiting for transfers between devices: 29.8 us -> 0.01 us  [body(): lax.all_to_all(grad_split, 'ctx', split_axis=1, concat_axis=0, tiled=True)]
    sub x36 -> x1, other arithmetic: 25.4 us -> 0.01 us  [body(): starts = bounds - lengths]
  transfers between devices with their start and end apart: 8 -> 8, of which waited for: 3 -> 6; matrix products, arithmetic and copies ran while one was open for 9% -> 7% of each run, Pallas kernels for 0% -> 0%
where the time goes in v1:
time: 367 us; the launch traced here: 366 us
  blocking collectives  141 us (38%)
  waiting for transfers between devices  79.8 us (22%)
  starting transfers between devices  62.4 us (17%)
  Pallas kernels  37.6 us (10%)
  local copies, waits for them, and re-layouts  32.3 us (9%)
  other arithmetic  11.8 us (3%)
    psum x1, blocking collectives, body(): bias_grads = lax.psum(bias_local, 'dp')  64.3 us
    all_gather x1, blocking collectives, body(): end_whole = lax.all_gather(subtree_end[0], 'ctx', axis=0, tiled=True)  43.1 us
    pallas_call x1, Pallas kernels, attention_grads(): pl.pallas_call(kernel, grid_spec=grid_spec, out_shape=[jax.ShapeDtypeStru...  37.6 us
    all_gather x1, blocking collectives, body(): depth_whole = lax.all_gather(depths[0], 'ctx', axis=0, tiled=True)  33.8 us
    all_to_all x1, waiting for transfers between devices, body(): lax.all_to_all(query_split, 'ctx', split_axis=1, concat_axis=0, tiled=True)  20.3 us
    unnamed x56, local copies, waits for them, and re-layouts  17.8 us
    all_to_all x1, waiting for transfers between devices, body(): lax.all_to_all(value_scaled.astype(jnp.bfloat16), 'ctx', split_axis=0, co...  15.7 us
    all_to_all x1, waiting for transfers between devices, body(): lax.all_to_all(key_rep, 'ctx', split_axis=1, concat_axis=0, tiled=True)  15 us
  transfers between devices with their start and end apart: 8, of which 6 were waited for; matrix products, arithmetic and copies ran while one was open for 7% of the time, Pallas kernels for 0%

profile of v1, /device:TPU:6, one launch (start us, length us, event | category | flops | bytes accessed | tf_op | source)
XLA Modules:
  0.0 366.1 jit_solution(15194842200989967861)
XLA Ops:
  0.6 1.8 multiply_bitcast_fusion
  4.1 10.1 %all-to-all-start.2 = ((f32[128,16,2]{0,2,1:T(2,128)}), f32[128,16,2]{0,2,1:T(2,128)S(1)}, u32[]{:S(2)}, u32[]{:S(2)}) async-start(f32[128,16,2]{0,2,1:T(2,128)} %bitcast.21), calls=%async_computation.2 | async-start | bytes 32768 | tf_op jit(solution)/shard_map/all_to_all | solution.py:233
  14.3 7.9 %all-to-all-done.2 = f32[128,16,2]{0,2,1:T(2,128)S(1)} async-done(((f32[128,16,2]{0,2,1:T(2,128)}), f32[128,16,2]{0,2,1:T(2,128)S(1)}, u32[]{:S(2)}, u32[]{:S(2)}) %all-to-all-start.2) | async-done | bytes 16416 | tf_op jit(solution)/shard_map/all_to_all | solution.py:233
  23.1 5.4 %all-to-all-start.3 = ((bf16[128,16,128]{0,2,1:T(8,128)(2,1)}), bf16[128,16,128]{0,2,1:T(8,128)(2,1)S(1)}, u32[]{:S(2)}, u32[]{:S(2)}) async-start(bf16[128,16,128]{0,2,1:T(8,128)(2,1)} %bitcast.26), calls=%async_computation.3 | async-start | bytes 1048576 | tf_op jit(solution)/shard_map/all_to_all | solution.py:244
  28.7 15.0 %all-to-all-done.3 = bf16[128,16,128]{0,2,1:T(8,128)(2,1)S(1)} async-done(((bf16[128,16,128]{0,2,1:T(8,128)(2,1)}), bf16[128,16,128]{0,2,1:T(8,128)(2,1)S(1)}, u32[]{:S(2)}, u32[]{:S(2)}) %all-to-all-start.3) | async-done | bytes 524320 | tf_op jit(solution)/shard_map/all_to_all | solution.py:244
  44.5 6.2 %all-to-all-start.4 = ((bf16[128,16,128]{0,2,1:T(8,128)(2,1)}), bf16[128,16,128]{0,2,1:T(8,128)(2,1)S(1)}, u32[]{:S(2)}, u32[]{:S(2)}) async-start(bf16[128,16,128]{0,2,1:T(8,128)(2,1)} %bitcast.31), calls=%async_computation.4 | async-start | bytes 1048576 | tf_op jit(solution)/shard_map/all_to_all | solution.py:245
  50.8 2.4 copy.109
  53.1 12.2 %all-to-all-done.4 = bf16[128,16,128]{0,2,1:T(8,128)(2,1)S(1)} async-done(((bf16[128,16,128]{0,2,1:T(8,128)(2,1)}), bf16[128,16,128]{0,2,1:T(8,128)(2,1)S(1)}, u32[]{:S(2)}, u32[]{:S(2)}) %all-to-all-start.4) | async-done | bytes 524320 | tf_op jit(solution)/shard_map/all_to_all | solution.py:245
  66.1 6.0 %all-to-all-start = ((bf16[128,16,256]{0,2,1:T(8,128)(2,1)}), bf16[128,16,256]{0,2,1:T(8,128)(2,1)S(1)}, u32[]{:S(2)}, u32[]{:S(2)}) async-start(bf16[128,16,256]{0,2,1:T(8,128)(2,1)} %bitcast.13), calls=%async_computation | async-start | bytes 2097152 | tf_op jit(solution)/shard_map/all_to_all | solution.py:238
  73.5 20.3 %all-to-all-done = bf16[128,16,256]{0,2,1:T(8,128)(2,1)S(1)} async-done(((bf16[128,16,256]{0,2,1:T(8,128)(2,1)}), bf16[128,16,256]{0,2,1:T(8,128)(2,1)S(1)}, u32[]{:S(2)}, u32[]{:S(2)}) %all-to-all-start) | async-done | bytes 1048608 | tf_op jit(solution)/shard_map/all_to_all | solution.py:238
  93.8 10.0 %all-to-all-start.1 = ((bf16[128,16,256]{0,2,1:T(8,128)(2,1)}), bf16[128,16,256]{0,2,1:T(8,128)(2,1)}, u32[]{:S(2)}, u32[]{:S(2)}) async-start(bf16[128,16,256]{0,2,1:T(8,128)(2,1)} %bitcast.17), calls=%async_computation.1 | async-start | bytes 2097152 | tf_op jit(solution)/shard_map/all_to_all | solution.py:239
  106.1 4.4 %compare_select_fusion.1 = (s32[2048,1]{0,1:T(1,128)S(1)}, s32[2048,1]{0,1:T(1,128)S(1)}) fusion(s32[]{:T(128)} %bitcast.5, s32[]{:T(128)} %bitcast.6, s32[]{:T(128)} %bitcast.7, s32[]{:T(128)} %bitcast.8, s32[]{:T(128)} %bitcast.9, s32[]{:T(128)} %bitcast.11, s32[]{:T(128)} %bitcast.10, s32[2048,1]{0,1:T(1,128)S(1)} %bitcast.124), kind=kLoop, calls=%fused_computation.12 | loop fusion | flops 32768 | bytes 24604 | tf_op jit(solution)/shard_map/gather | solution.py:224
  111.4 33.8 %all-gather.drow_ref = s32[1,2048]{1,0:T(1,128)S(1)} all-gather(s32[1,128]{1,0:T(1,128)S(1)} %copy-done.12), channel_id=2, replica_groups=mesh['dp'=32,'ctx'=16] {'ctx'}, dimensions={1}, use_global_device_ids=true | all-gather | bytes 8704 | tf_op jit(solution)/shard_map/all_gather | solution.py:217
  146.6 43.1 %all-gather.1.erow_ref = s32[1,2048]{1,0:T(1,128)S(1)} all-gather(s32[1,128]{1,0:T(1,128)S(1)} %copy-done.13), channel_id=3, replica_groups=mesh['dp'=32,'ctx'=16] {'ctx'}, dimensions={1}, use_global_device_ids=true | all-gather | bytes 8704 | tf_op jit(solution)/shard_map/all_gather | solution.py:218
  194.7 1.9 copy.112
  196.9 1.4 copy.120.do_ref
  199.3 37.6 %shard_map.129 = (bf16[2048,256]{1,0:T(8,128)(2,1)S(1)}, f32[128,2048]{1,0:T(8,128)S(1)}, f32[128,2048]{1,0:T(8,128)S(1)}, f32[4,1,256]{2,1,0:T(1,128)S(1)}) custom-call(s32[8]{0:T(128)S(1)} %and_select_fusion.lo_ref, f32[4]{0:T(128)S(1)} %pad_maximum_fusion.1.sg_ref, bf16[2048,256]{1,0:T(8,128)(2,1)S(1)} %copy.119.q_ref, bf16[256,2048]{1,0:T(8,128)(2,1)} %bitcast.131, ...), custom_call_target="tpu_custom_call" | custom-call | flops 6039797760 | bytes 6291456 | tf_op jit(solution)/shard_map/pallas_call | solution.py:169
  239.8 10.4 %all-to-all-start.7 = ((bf16[16,2,8192]{2,1,0:T(2,128)(2,1)}), bf16[16,2,8192]{2,1,0:T(2,128)(2,1)S(1)}, u32[]{:S(2)}, u32[]{:S(2)}) async-start(bf16[16,2,8192]{2,1,0:T(2,128)(2,1)} %reshape.196), calls=%async_computation.7 | async-start | bytes 1048576 | tf_op jit(solution)/shard_map/all_to_all | solution.py:276
  252.4 15.7 %all-to-all-done.7 = bf16[16,2,8192]{2,1,0:T(2,128)(2,1)S(1)} async-done(((bf16[16,2,8192]{2,1,0:T(2,128)(2,1)}), bf16[16,2,8192]{2,1,0:T(2,128)(2,1)S(1)}, u32[]{:S(2)}, u32[]{:S(2)}) %all-to-all-start.7) | async-done | bytes 524320 | tf_op jit(solution)/shard_map/all_to_all | solution.py:276
  268.1 8.7 %all-to-all-start.6 = ((bf16[16,2,8192]{2,1,0:T(2,128)(2,1)}), bf16[16,2,8192]{2,1,0:T(2,128)(2,1)S(1)}, u32[]{:S(2)}, u32[]{:S(2)}) async-start(bf16[16,2,8192]{2,1,0:T(2,128)(2,1)} %reshape.194), calls=%async_computation.6 | async-start | bytes 1048576 | tf_op jit(solution)/shard_map/all_to_all | solution.py:273
  276.7 1.4 reduce.4
  279.3 8.7 %all-to-all-done.6 = bf16[16,2,8192]{2,1,0:T(2,128)(2,1)S(1)} async-done(((bf16[16,2,8192]{2,1,0:T(2,128)(2,1)}), bf16[16,2,8192]{2,1,0:T(2,128)(2,1)S(1)}, u32[]{:S(2)}, u32[]{:S(2)}) %all-to-all-start.6) | async-done | bytes 524320 | tf_op jit(solution)/shard_map/all_to_all | solution.py:273
  288.8 5.7 %all-to-all-start.5 = ((bf16[16,2,16384]{2,1,0:T(2,128)(2,1)}), bf16[16,2,16384]{2,1,0:T(2,128)(2,1)S(1)}, u32[]{:S(2)}, u32[]{:S(2)}) async-start(bf16[16,2,16384]{2,1,0:T(2,128)(2,1)} %reshape.192), calls=%async_computation.5 | async-start | bytes 2097152 | tf_op jit(solution)/shard_map/all_to_all | solution.py:267
  294.7 64.3 %psum.7 = f32[2,2]{0,1:T(2,128)S(1)} all-reduce(f32[2,2]{0,1:T(2,128)S(1)} %pad_maximum_fusion), channel_id=1, replica_groups=mesh['dp'=32,'ctx'=16] {'dp'}, use_global_device_ids=true, to_apply=%region_6.7 | all-reduce | flops 4 | bytes 32 | tf_op jit(solution)/shard_map/psum | solution.py:285
  (94 shorter events, 30.9 us)
Async XLA Ops:
  2.8 11.4 %copy-start.10 = (bf16[1,128,512]{2,1,0:T(8,128)(2,1)S(1)}, bf16[1,128,512]{2,1,0:T(8,128)(2,1)}, u32[]{:S(2)}) copy-start(bf16[1,128,512]{2,1,0:T(8,128)(2,1)} %param.11) | copy-start | bytes 393220
  2.8 25.7 %copy-start.11 = (bf16[1,128,512]{2,1,0:T(8,128)(2,1)S(1)}, bf16[1,128,512]{2,1,0:T(8,128)(2,1)}, u32[]{:S(2)}) copy-start(bf16[1,128,512]{2,1,0:T(8,128)(2,1)} %param.12) | copy-start | bytes 393220
  4.1 18.1 %all-to-all-start.2 = ((f32[128,16,2]{0,2,1:T(2,128)}), f32[128,16,2]{0,2,1:T(2,128)S(1)}, u32[]{:S(2)}, u32[]{:S(2)}) async-start(f32[128,16,2]{0,2,1:T(2,128)} %bitcast.21), calls=%async_computation.2 | async-start | bytes 32768 | tf_op jit(solution)/shard_map/all_to_all | solution.py:233
  23.1 20.5 %all-to-all-start.3 = ((bf16[128,16,128]{0,2,1:T(8,128)(2,1)}), bf16[128,16,128]{0,2,1:T(8,128)(2,1)S(1)}, u32[]{:S(2)}, u32[]{:S(2)}) async-start(bf16[128,16,128]{0,2,1:T(8,128)(2,1)} %bitcast.26), calls=%async_computation.3 | async-start | bytes 1048576 | tf_op jit(solution)/shard_map/all_to_all | solution.py:244
  44.5 20.8 %all-to-all-start.4 = ((bf16[128,16,128]{0,2,1:T(8,128)(2,1)}), bf16[128,16,128]{0,2,1:T(8,128)(2,1)S(1)}, u32[]{:S(2)}, u32[]{:S(2)}) async-start(bf16[128,16,128]{0,2,1:T(8,128)(2,1)} %bitcast.31), calls=%async_computation.4 | async-start | bytes 1048576 | tf_op jit(solution)/shard_map/all_to_all | solution.py:245
  50.7 21.4 %copy-start.3 = (bf16[1,128,4096]{2,1,0:T(8,128)(2,1)S(1)}, bf16[1,128,4096]{2,1,0:T(8,128)(2,1)}, u32[]{:S(2)}) copy-start(bf16[1,128,4096]{2,1,0:T(8,128)(2,1)} %param.14) | copy-start | bytes 3145732
  65.3 0.8 copy-start.8
  66.1 27.7 %all-to-all-start = ((bf16[128,16,256]{0,2,1:T(8,128)(2,1)}), bf16[128,16,256]{0,2,1:T(8,128)(2,1)S(1)}, u32[]{:S(2)}, u32[]{:S(2)}) async-start(bf16[128,16,256]{0,2,1:T(8,128)(2,1)} %bitcast.13), calls=%async_computation | async-start | bytes 2097152 | tf_op jit(solution)/shard_map/all_to_all | solution.py:238
  72.1 31.6 %copy-start.14 = (s32[1,8]{1,0:T(1,128)S(1)}, s32[1,8]{1,0:T(1,128)}, u32[]{:S(2)}) copy-start(s32[1,8]{1,0:T(1,128)} %param.17) | copy-start | bytes 100
  73.5 37.8 %copy-start.15 = (f32[32]{0:T(128)S(1)}, f32[32]{0:T(128)}, u32[]{:S(2)}) copy-start(f32[32]{0:T(128)} %param.18) | copy-start | bytes 388
  73.5 37.9 %copy-start.16 = (f32[32]{0:T(128)S(1)}, f32[32]{0:T(128)}, u32[]{:S(2)}) copy-start(f32[32]{0:T(128)} %param.19) | copy-start | bytes 388
  73.5 38.0 %copy-start.12 = (s32[1,128]{1,0:T(1,128)S(1)}, s32[1,128]{1,0:T(1,128)}, u32[]{:S(2)}) copy-start(s32[1,128]{1,0:T(1,128)} %param.15) | copy-start | bytes 1540
  93.8 52.8 %copy-start.13 = (s32[1,128]{1,0:T(1,128)S(1)}, s32[1,128]{1,0:T(1,128)}, u32[]{:S(2)}) copy-start(s32[1,128]{1,0:T(1,128)} %param.16) | copy-start | bytes 1540
  93.8 100.9 %all-to-all-start.1 = ((bf16[128,16,256]{0,2,1:T(8,128)(2,1)}), bf16[128,16,256]{0,2,1:T(8,128)(2,1)}, u32[]{:S(2)}, u32[]{:S(2)}) async-start(bf16[128,16,256]{0,2,1:T(8,128)(2,1)} %bitcast.17), calls=%async_computation.1 | async-start | bytes 2097152 | tf_op jit(solution)/shard_map/all_to_all | solution.py:239
  189.8 2.1 copy-start.9
  194.2 2.5 copy-start.1
  196.9 1.4 copy-start.2
  198.3 1.0 copy-start
  239.8 28.3 %all-to-all-start.7 = ((bf16[16,2,8192]{2,1,0:T(2,128)(2,1)}), bf16[16,2,8192]{2,1,0:T(2,128)(2,1)S(1)}, u32[]{:S(2)}, u32[]{:S(2)}) async-start(bf16[16,2,8192]{2,1,0:T(2,128)(2,1)} %reshape.196), calls=%async_computation.7 | async-start | bytes 1048576 | tf_op jit(solution)/shard_map/all_to_all | solution.py:276
  268.1 11.2 %copy-start.4 = (bf16[16,2,8192]{2,1,0:T(2,128)(2,1)}, bf16[16,2,8192]{2,1,0:T(2,128)(2,1)S(1)}, u32[]{:S(2)}) copy-start(bf16[16,2,8192]{2,1,0:T(2,128)(2,1)S(1)} %all-to-all-done.7) | copy-start | bytes 1572868
  268.1 20.0 %all-to-all-start.6 = ((bf16[16,2,8192]{2,1,0:T(2,128)(2,1)}), bf16[16,2,8192]{2,1,0:T(2,128)(2,1)S(1)}, u32[]{:S(2)}, u32[]{:S(2)}) async-start(bf16[16,2,8192]{2,1,0:T(2,128)(2,1)} %reshape.194), calls=%async_computation.6 | async-start | bytes 1048576 | tf_op jit(solution)/shard_map/all_to_all | solution.py:273
  288.0 71.6 %copy-start.5 = (bf16[16,2,8192]{2,1,0:T(2,128)(2,1)S(1)}, bf16[16,2,8192]{2,1,0:T(2,128)(2,1)}, u32[]{:S(2)}) copy-start(bf16[16,2,8192]{2,1,0:T(2,128)(2,1)} %copy-done.4) | copy-start | bytes 1572868
  288.8 74.1 %all-to-all-start.5 = ((bf16[16,2,16384]{2,1,0:T(2,128)(2,1)}), bf16[16,2,16384]{2,1,0:T(2,128)(2,1)S(1)}, u32[]{:S(2)}, u32[]{:S(2)}) async-start(bf16[16,2,16384]{2,1,0:T(2,128)(2,1)} %reshape.192), calls=%async_computation.5 | async-start | bytes 2097152 | tf_op jit(solution)/shard_map/all_to_all | solution.py:267
  359.7 1.6 copy-start.7
  (1 other events, 0.8 us)

commit v2 on v1

--- a/solution.py
+++ b/solution.py
@@ -214,8 +214,6 @@
     local_slopes = lax.dynamic_slice_in_dim(slopes, head_first, local_heads)
     local_gains = lax.dynamic_slice_in_dim(ancestor_gain, head_first, local_heads)
     sg = jnp.concatenate([local_slopes, local_gains])
-    depth_whole = lax.all_gather(depths[0], "ctx", axis=0, tiled=True)
-    end_whole = lax.all_gather(subtree_end[0], "ctx", axis=0, tiled=True)
     positions = jnp.arange(seq_len, dtype=jnp.int32)
     lengths = file_lengths[0]
     bounds = jnp.cumsum(lengths)
@@ -230,21 +228,38 @@
         ),
         axis=2,
     )
-    delta_heads = lax.all_to_all(
-        delta_tok.reshape(tokens_here, context_size, local_heads), "ctx", split_axis=1, concat_axis=0, tiled=True
-    ).reshape(seq_len, local_heads)
-    query_split = queries[0].reshape(tokens_here, context_size, local_heads * HEAD_WIDTH)
-    grad_split = out_grads[0].reshape(tokens_here, context_size, local_heads * HEAD_WIDTH)
-    query_heads = lax.all_to_all(query_split, "ctx", split_axis=1, concat_axis=0, tiled=True)
-    grad_heads = lax.all_to_all(grad_split, "ctx", split_axis=1, concat_axis=0, tiled=True)
-    query_heads = query_heads.reshape(seq_len, local_heads * HEAD_WIDTH)
-    grad_heads = grad_heads.reshape(seq_len, local_heads * HEAD_WIDTH)
-    key_rep = jnp.repeat(key_rows[0].reshape(tokens_here, kv_heads, HEAD_WIDTH), repeats, axis=1)
-    value_rep = jnp.repeat(values[0].reshape(tokens_here, kv_heads, HEAD_WIDTH), repeats, axis=1)
-    key_head = lax.all_to_all(key_rep, "ctx", split_axis=1, concat_axis=0, tiled=True).reshape(seq_len, HEAD_WIDTH)
-    value_head = lax.all_to_all(value_rep, "ctx", split_axis=1, concat_axis=0, tiled=True).reshape(
-        seq_len, HEAD_WIDTH
-    )
+    tree_tok = jnp.stack([depths[0], subtree_end[0]], axis=1).astype(jnp.float32)
+    small_pack = jnp.concatenate(
+        [
+            delta_tok.reshape(tokens_here, context_size, local_heads),
+            jnp.broadcast_to(tree_tok[:, None, :], (tokens_here, context_size, 2)),
+        ],
+        axis=2,
+    )
+    small_heads = lax.all_to_all(small_pack, "ctx", split_axis=1, concat_axis=0, tiled=True).reshape(
+        seq_len, local_heads + 2
+    )
+    delta_heads = small_heads[:, :local_heads]
+    depth_whole = small_heads[:, local_heads].astype(jnp.int32)
+    end_whole = small_heads[:, local_heads + 1].astype(jnp.int32)
+
+    width = local_heads * HEAD_WIDTH
+    big_pack = jnp.concatenate(
+        [
+            queries[0].reshape(tokens_here, context_size, width),
+            out_grads[0].reshape(tokens_here, context_size, width),
+            jnp.repeat(key_rows[0].reshape(tokens_here, kv_heads, HEAD_WIDTH), repeats, axis=1),
+            jnp.repeat(values[0].reshape(tokens_here, kv_heads, HEAD_WIDTH), repeats, axis=1),
+        ],
+        axis=2,
+    )
+    big_heads = lax.all_to_all(big_pack, "ctx", split_axis=1, concat_axis=0, tiled=True).reshape(
+        seq_len, 2 * width + 2 * HEAD_WIDTH
+    )
+    query_heads = big_heads[:, :width]
+    grad_heads = big_heads[:, width : 2 * width]
+    key_head = big_heads[:, 2 * width : 2 * width + HEAD_WIDTH]
+    value_head = big_heads[:, 2 * width + HEAD_WIDTH :]
 
     dq, dkT, dvT, bias_part = attention_grads(
         query_heads,
@@ -264,25 +279,24 @@
         sg,
     )
 
-    query_back = lax.all_to_all(
-        dq.reshape(seq_len, 1, local_heads * HEAD_WIDTH), "ctx", split_axis=0, concat_axis=1, tiled=True
-    )
-    query_grads = query_back.reshape(1, tokens_here, heads_all * HEAD_WIDTH)
-    key_scaled = (dkT.T * factor).reshape(seq_len, 1, HEAD_WIDTH)
-    value_scaled = dvT.T.reshape(seq_len, 1, HEAD_WIDTH)
-    key_back = lax.all_to_all(
-        key_scaled.astype(jnp.bfloat16), "ctx", split_axis=0, concat_axis=1, tiled=True
-    ).astype(jnp.float32)
-    value_back = lax.all_to_all(
-        value_scaled.astype(jnp.bfloat16), "ctx", split_axis=0, concat_axis=1, tiled=True
-    ).astype(jnp.float32)
+    back_pack = jnp.concatenate(
+        [dq, (dkT.T * factor).astype(jnp.bfloat16), dvT.T.astype(jnp.bfloat16)], axis=1
+    ).reshape(seq_len, 1, width + 2 * HEAD_WIDTH)
+    back = lax.all_to_all(back_pack, "ctx", split_axis=0, concat_axis=1, tiled=True)
+    query_grads = back[:, :, :width].reshape(1, tokens_here, heads_all * HEAD_WIDTH)
+    key_back = back[:, :, width : width + HEAD_WIDTH].astype(jnp.float32)
+    value_back = back[:, :, width + HEAD_WIDTH :].astype(jnp.float32)
     key_grads = jnp.sum(key_back.reshape(tokens_here, kv_heads, repeats, HEAD_WIDTH), axis=2)
     value_grads = jnp.sum(value_back.reshape(tokens_here, kv_heads, repeats, HEAD_WIDTH), axis=2)
     key_grads = key_grads.astype(jnp.bfloat16).reshape(1, tokens_here, kv_heads * HEAD_WIDTH)
     value_grads = value_grads.astype(jnp.bfloat16).reshape(1, tokens_here, kv_heads * HEAD_WIDTH)
     bias_sums = jnp.sum(bias_part, axis=(1, 2))
     bias_local = jnp.stack([-bias_sums[:local_heads], bias_sums[local_heads:]], axis=1)
-    bias_grads = lax.psum(bias_local, "dp")
+    bias_slots = lax.dynamic_update_slice_in_dim(
+        jnp.zeros((heads_all, 2), jnp.float32), bias_local, head_first, 0
+    )
+    bias_total = lax.psum(bias_slots, ("dp", "ctx"))
+    bias_grads = lax.dynamic_slice_in_dim(bias_total, head_first, local_heads, 0)
     return (query_grads, key_grads, value_grads, bias_grads)
 
 

time: 367 us -> 326 us (0.89)
  starting transfers between devices: 62.4 us -> 22.9 us
  waiting for transfers between devices: 79.8 us -> 67.3 us
  other arithmetic: 11.8 us -> 19 us
  local copies, waits for them, and re-layouts: 32.3 us -> 37.9 us
    all_gather x2 -> x0, blocking collectives: 76.9 us -> none  [the longest x1 43.1 us: body(): end_whole = lax.all_gather(subtree_end[0], 'ctx', axis=0, tiled=True)]
    psum x1, blocking collectives: 64.3 us -> 138 us  [body(): bias_total = lax.psum(bias_slots, ('dp', 'ctx'))]
    all_to_all x8 -> x3, starting transfers between devices: 62.4 us -> 22.9 us  [the longest x1 10.1 us: body(): lax.all_to_all(small_pack, 'ctx', split_axis=1, concat_axis=0, tiled=True)]
    all_to_all x8 -> x3, waiting for transfers between devices: 79.8 us -> 67.3 us  [the longest x1 63.9 us: body(): lax.all_to_all(big_pack, 'ctx', split_axis=1, concat_axis=0, tiled=True)]
    slice x0 -> x5, local copies, waits for them, and re-layouts: none -> 5.61 us  [the longest x1 2.06 us: body(): key_head = big_heads[:, 2 * width:2 * width + HEAD_WIDTH]]
    reshape x1 -> x2, other arithmetic: 1.45 us -> 5.47 us  [body(): back_pack = jnp.concatenate([dq, (dkT.T * factor).astype(jnp.bfloat16), d...]
    unnamed x56 -> x30, local copies, waits for them, and re-layouts: 17.8 us -> 20.3 us
  transfers between devices with their start and end apart: 8 -> 3, of which waited for: 6 -> 2; matrix products, arithmetic and copies ran while one was open for 7% -> 5% of each run, Pallas kernels for 0% -> 0%
where the time goes in v2:
time: 326 us; the launch traced here: 324 us
  blocking collectives  138 us (42%)
  waiting for transfers between devices  67.3 us (21%)
  local copies, waits for them, and re-layouts  37.9 us (12%)
  Pallas kernels  37.6 us (12%)
  starting transfers between devices  22.9 us (7%)
  other arithmetic  19 us (6%)
    psum x1, blocking collectives, body(): bias_total = lax.psum(bias_slots, ('dp', 'ctx'))  138 us
    all_to_all x1, waiting for transfers between devices, body(): lax.all_to_all(big_pack, 'ctx', split_axis=1, concat_axis=0, tiled=True)  63.9 us
    pallas_call x1, Pallas kernels, attention_grads(): pl.pallas_call(kernel, grid_spec=grid_spec, out_shape=[jax.ShapeDtypeStru...  37.6 us
    unnamed x30, local copies, waits for them, and re-layouts  20.3 us
    all_to_all x1, starting transfers between devices, body(): lax.all_to_all(small_pack, 'ctx', split_axis=1, concat_axis=0, tiled=True)  10.1 us
    all_to_all x1, starting transfers between devices, body(): lax.all_to_all(back_pack, 'ctx', split_axis=0, concat_axis=1, tiled=True)  6.57 us
  transfers between devices with their start and end apart: 3, of which 2 were waited for; matrix products, arithmetic and copies ran while one was open for 5% of the time, Pallas kernels for 0%

profile of v2, /device:TPU:6, one launch (start us, length us, event | category | flops | bytes accessed | tf_op | source)
XLA Modules:
  0.0 323.9 jit_solution(7866986813303877167)
XLA Ops:
  0.6 1.8 multiply_bitcast_fusion
  4.2 10.1 %all-to-all-start.1 = ((f32[128,16,4]{0,2,1:T(4,128)}), f32[128,16,4]{0,2,1:T(4,128)S(1)}, u32[]{:S(2)}, u32[]{:S(2)}) async-start(f32[128,16,4]{0,2,1:T(4,128)} %pad_maximum_fusion.1), calls=%async_computation.1 | async-start | bytes 65536 | tf_op jit(solution)/shard_map/all_to_all | solution.py:239
  15.0 1.6 copy.95
  17.1 1.8 pad_maximum_fusion
  18.9 3.5 %all-to-all-done.1 = f32[128,16,4]{0,2,1:T(4,128)S(1)} async-done(((f32[128,16,4]{0,2,1:T(4,128)}), f32[128,16,4]{0,2,1:T(4,128)S(1)}, u32[]{:S(2)}, u32[]{:S(2)}) %all-to-all-start.1) | async-done | bytes 32800 | tf_op jit(solution)/shard_map/all_to_all | solution.py:239
  22.4 6.3 %all-to-all-start = ((bf16[128,16,768]{0,2,1:T(8,128)(2,1)}), bf16[128,16,768]{0,2,1:T(8,128)(2,1)}, u32[]{:S(2)}, u32[]{:S(2)}) async-start(bf16[128,16,768]{0,2,1:T(8,128)(2,1)} %pad_maximum_fusion), calls=%async_computation | async-start | bytes 6291456 | tf_op jit(solution)/shard_map/all_to_all | solution.py:256
  29.0 1.4 copy.105.fcol_ref
  31.0 4.5 %compare_select_fusion.1 = (s32[2048,1]{0,1:T(1,128)S(1)}, s32[2048,1]{0,1:T(1,128)S(1)}) fusion(s32[]{:T(128)} %bitcast.5, s32[]{:T(128)} %bitcast.6, s32[]{:T(128)} %bitcast.7, s32[]{:T(128)} %bitcast.8, s32[]{:T(128)} %bitcast.9, s32[]{:T(128)} %bitcast.11, s32[]{:T(128)} %bitcast.10, s32[2048,1]{0,1:T(1,128)S(1)} %bitcast.77), kind=kLoop, calls=%fused_computation.18 | loop fusion | flops 32768 | bytes 24604 | tf_op jit(solution)/shard_map/gather | solution.py:222
  38.2 1.4 slice_convert_fusion.1.dcol_ref
  39.6 63.9 %all-to-all-done = bf16[128,16,768]{0,2,1:T(8,128)(2,1)} async-done(((bf16[128,16,768]{0,2,1:T(8,128)(2,1)}), bf16[128,16,768]{0,2,1:T(8,128)(2,1)}, u32[]{:S(2)}, u32[]{:S(2)}) %all-to-all-start) | async-done | bytes 3145760 | tf_op jit(solution)/shard_map/all_to_all | solution.py:256
  103.4 3.9 %copy.99 = bf16[16,128,1,768]{1,0,3,2:T(8,128)(2,1)S(1)} copy(bf16[16,128,1,768]{1,3,0,2:T(8,128)(2,1)} %bitcast.20) | data formatting | bytes 6291456 | tf_op jit(solution)/shard_map/all_to_all | solution.py:256
  108.7 1.9 slice_bitcast_fusion.3
  111.6 1.5 copy.102.q_ref
  113.1 1.3 copy.103.do_ref
  114.4 2.1 copy.104.k_ref
  117.5 37.6 %shard_map.129 = (bf16[2048,256]{1,0:T(8,128)(2,1)S(1)}, f32[128,2048]{1,0:T(8,128)S(1)}, f32[128,2048]{1,0:T(8,128)S(1)}, f32[4,1,256]{2,1,0:T(1,128)S(1)}) custom-call(s32[8]{0:T(128)S(1)} %and_select_fusion.lo_ref, f32[4]{0:T(128)S(1)} %pad_maximum_fusion.3.sg_ref, bf16[2048,256]{1,0:T(8,128)(2,1)S(1)} %copy.102.q_ref, ...), custom_call_target="tpu_custom_call" | custom-call | flops 6039797760 | bytes 6291456 | tf_op jit(solution)/shard_map/pallas_call | solution.py:169
  155.9 1.6 maximum_bitcast_fusion
  157.9 3.9 %reduce.10 = bf16[2048,512]{1,0:T(8,128)(2,1)S(1)} reduce(bf16[2048,1,512]{2,0,1:T(8,128)(2,1)} %maximum_bitcast_fusion, bf16[]{:T(256)} %broadcast.100), dimensions={1}, to_apply=%copy.108.reduce_sub_computation | reduce | bytes 4194306 | tf_op jit(solution)/shard_map/reshape | solution.py:284
  161.8 2.8 reshape.212
  164.6 6.6 %all-to-all-start.2 = ((bf16[16,2,32768]{2,1,0:T(2,128)(2,1)}), bf16[16,2,32768]{2,1,0:T(2,128)(2,1)S(1)}, u32[]{:S(2)}, u32[]{:S(2)}) async-start(bf16[16,2,32768]{2,1,0:T(2,128)(2,1)} %reshape.212), calls=%async_computation.2 | async-start | bytes 4194304 | tf_op jit(solution)/shard_map/all_to_all | solution.py:285
  171.5 138.2 %psum.7 = f32[32,2]{1,0:T(8,128)S(1)} all-reduce(f32[32,2]{1,0:T(8,128)S(1)} %constant_dynamic-update-slice_fusion), channel_id=1, replica_groups=mesh['dp'=32,'ctx'=16] {'dp','ctx'}, use_global_device_ids=true, to_apply=%region_6.7 | all-reduce | flops 64 | bytes 512 | tf_op jit(solution)/shard_map/psum | solution.py:298
  310.3 6.8 %reshape.213 = bf16[2048,1,512]{2,1,0:T(2,128)(2,1)} reshape(bf16[16,2,32768]{2,1,0:T(2,128)(2,1)S(1)} %all-to-all-done.2) | data formatting | bytes 4194304
  317.1 2.8 copy.118
  320.8 1.3 copy.113
  (65 shorter events, 14.5 us)
Async XLA Ops:
  2.4 1.1 copy-start.5
  2.4 1.1 copy-start.6
  2.5 11.8 %copy-start.2 = (bf16[1,128,4096]{2,1,0:T(8,128)(2,1)S(1)}, bf16[1,128,4096]{2,1,0:T(8,128)(2,1)}, u32[]{:S(2)}) copy-start(bf16[1,128,4096]{2,1,0:T(8,128)(2,1)} %param.14) | copy-start | bytes 3145732
  2.8 13.7 %copy-start.3 = (bf16[1,128,512]{2,1,0:T(8,128)(2,1)S(1)}, bf16[1,128,512]{2,1,0:T(8,128)(2,1)}, u32[]{:S(2)}) copy-start(bf16[1,128,512]{2,1,0:T(8,128)(2,1)} %param.11) | copy-start | bytes 393220
  2.9 13.9 %copy-start.4 = (bf16[1,128,512]{2,1,0:T(8,128)(2,1)S(1)}, bf16[1,128,512]{2,1,0:T(8,128)(2,1)}, u32[]{:S(2)}) copy-start(bf16[1,128,512]{2,1,0:T(8,128)(2,1)} %param.12) | copy-start | bytes 393220
  4.2 18.2 %all-to-all-start.1 = ((f32[128,16,4]{0,2,1:T(4,128)}), f32[128,16,4]{0,2,1:T(4,128)S(1)}, u32[]{:S(2)}, u32[]{:S(2)}) async-start(f32[128,16,4]{0,2,1:T(4,128)} %pad_maximum_fusion.1), calls=%async_computation.1 | async-start | bytes 65536 | tf_op jit(solution)/shard_map/all_to_all | solution.py:239
  18.9 9.8 %copy-start.7 = (s32[1,8]{1,0:T(1,128)S(1)}, s32[1,8]{1,0:T(1,128)}, u32[]{:S(2)}) copy-start(s32[1,8]{1,0:T(1,128)} %param.17) | copy-start | bytes 100
  18.9 17.5 %copy-start.8 = (f32[32]{0:T(128)S(1)}, f32[32]{0:T(128)}, u32[]{:S(2)}) copy-start(f32[32]{0:T(128)} %param.19) | copy-start | bytes 388
  18.9 17.5 %copy-start.9 = (f32[32]{0:T(128)S(1)}, f32[32]{0:T(128)}, u32[]{:S(2)}) copy-start(f32[32]{0:T(128)} %param.18) | copy-start | bytes 388
  22.4 81.0 %all-to-all-start = ((bf16[128,16,768]{0,2,1:T(8,128)(2,1)}), bf16[128,16,768]{0,2,1:T(8,128)(2,1)}, u32[]{:S(2)}, u32[]{:S(2)}) async-start(bf16[128,16,768]{0,2,1:T(8,128)(2,1)} %pad_maximum_fusion), calls=%async_computation | async-start | bytes 6291456 | tf_op jit(solution)/shard_map/all_to_all | solution.py:256
  37.0 70.4 %copy-start.1 = (f32[16,128,1,4]{3,1,0,2:T(8,128)}, f32[16,128,1,4]{3,1,0,2:T(8,128)S(1)}, u32[]{:S(2)}) copy-start(f32[16,128,1,4]{3,1,0,2:T(8,128)S(1)} %copy.101) | copy-start | bytes 98308
  116.5 1.0 copy-start
  164.6 145.7 %all-to-all-start.2 = ((bf16[16,2,32768]{2,1,0:T(2,128)(2,1)}), bf16[16,2,32768]{2,1,0:T(2,128)(2,1)S(1)}, u32[]{:S(2)}, u32[]{:S(2)}) async-start(bf16[16,2,32768]{2,1,0:T(2,128)(2,1)} %reshape.212), calls=%async_computation.2 | async-start | bytes 4194304 | tf_op jit(solution)/shard_map/all_to_all | solution.py:285

commit v3 on v2

--- a/solution.py
+++ b/solution.py
@@ -292,11 +292,10 @@
     value_grads = value_grads.astype(jnp.bfloat16).reshape(1, tokens_here, kv_heads * HEAD_WIDTH)
     bias_sums = jnp.sum(bias_part, axis=(1, 2))
     bias_local = jnp.stack([-bias_sums[:local_heads], bias_sums[local_heads:]], axis=1)
-    bias_slots = lax.dynamic_update_slice_in_dim(
-        jnp.zeros((heads_all, 2), jnp.float32), bias_local, head_first, 0
-    )
-    bias_total = lax.psum(bias_slots, ("dp", "ctx"))
-    bias_grads = lax.dynamic_slice_in_dim(bias_total, head_first, local_heads, 0)
+    data_size = lax.axis_size("dp")
+    bias_copies = jnp.broadcast_to(bias_local[None], (data_size, local_heads, 2))
+    bias_each = lax.all_to_all(bias_copies, "dp", split_axis=0, concat_axis=0, tiled=True)
+    bias_grads = jnp.sum(bias_each, axis=0)
     return (query_grads, key_grads, value_grads, bias_grads)
 
 

time: 326 us -> 260 us (0.80)
  the two profiles are of different devices: /device:TPU:6 before, /device:TPU:8 now
where the time goes in v3:
time: 260 us; the launch traced here: 259 us
  waiting for transfers between devices  116 us (45%)
  local copies, waits for them, and re-layouts  45.5 us (18%)
  starting transfers between devices  40 us (15%)
  Pallas kernels  37.5 us (14%)
  other arithmetic  19.5 us (8%)
    all_to_all x1, waiting for transfers between devices, body(): lax.all_to_all(big_pack, 'ctx', split_axis=1, concat_axis=0, tiled=True)  55.5 us
    all_to_all x1, waiting for transfers between devices, body(): lax.all_to_all(back_pack, 'ctx', split_axis=0, concat_axis=1, tiled=True)  55 us
    pallas_call x1, Pallas kernels, attention_grads(): pl.pallas_call(kernel, grid_spec=grid_spec, out_shape=[jax.ShapeDtypeStru...  37.5 us
    unnamed x38, local copies, waits for them, and re-layouts  25 us
    all_to_all x1, starting transfers between devices, body(): lax.all_to_all(bias_copies, 'dp', split_axis=0, concat_axis=0, tiled=True)  22.8 us
    all_to_all x1, starting transfers between devices, body(): lax.all_to_all(small_pack, 'ctx', split_axis=1, concat_axis=0, tiled=True)  8.77 us
    all_to_all x1, waiting for transfers between devices, body(): lax.all_to_all(small_pack, 'ctx', split_axis=1, concat_axis=0, tiled=True)  5.38 us
    gather x3, other arithmetic, body(): file_start = starts[jnp.minimum(file_whole, lengths.shape[0] - 1)]  5.21 us
  transfers between devices with their start and end apart: 4, of which 3 were waited for; matrix products, arithmetic and copies ran while one was open for 12% of the time, Pallas kernels for 0%

profile of v3, /device:TPU:8, one launch (start us, length us, event | category | flops | bytes accessed | tf_op | source)
XLA Modules:
  0.0 259.3 jit_solution(11988961904528327324)
XLA Ops:
  0.6 1.8 multiply_bitcast_fusion
  4.2 8.8 %all-to-all-start.1 = ((f32[128,16,4]{0,2,1:T(4,128)}), f32[128,16,4]{0,2,1:T(4,128)S(1)}, u32[]{:S(2)}, u32[]{:S(2)}) async-start(f32[128,16,4]{0,2,1:T(4,128)} %pad_maximum_fusion.1), calls=%async_computation.1 | async-start | bytes 65536 | tf_op jit(solution)/shard_map/all_to_all | solution.py:239
  13.7 1.6 copy.116
  15.8 1.8 pad_maximum_fusion
  17.6 5.4 %all-to-all-done.1 = f32[128,16,4]{0,2,1:T(4,128)S(1)} async-done(((f32[128,16,4]{0,2,1:T(4,128)}), f32[128,16,4]{0,2,1:T(4,128)S(1)}, u32[]{:S(2)}, u32[]{:S(2)}) %all-to-all-start.1) | async-done | bytes 32800 | tf_op jit(solution)/shard_map/all_to_all | solution.py:239
  23.0 4.5 %all-to-all-start = ((bf16[128,16,768]{0,2,1:T(8,128)(2,1)}), bf16[128,16,768]{0,2,1:T(8,128)(2,1)}, u32[]{:S(2)}, u32[]{:S(2)}) async-start(bf16[128,16,768]{0,2,1:T(8,128)(2,1)} %pad_maximum_fusion), calls=%async_computation | async-start | bytes 6291456 | tf_op jit(solution)/shard_map/all_to_all | solution.py:256
  27.8 1.4 copy.126.fcol_ref
  29.9 4.5 %compare_select_fusion.1 = (s32[2048,1]{0,1:T(1,128)S(1)}, s32[2048,1]{0,1:T(1,128)S(1)}) fusion(s32[]{:T(128)} %bitcast.5, s32[]{:T(128)} %bitcast.6, s32[]{:T(128)} %bitcast.7, s32[]{:T(128)} %bitcast.8, s32[]{:T(128)} %bitcast.9, s32[]{:T(128)} %bitcast.11, s32[]{:T(128)} %bitcast.10, s32[2048,1]{0,1:T(1,128)S(1)} %bitcast.77), kind=kLoop, calls=%fused_computation.18 | loop fusion | flops 32768 | bytes 24604 | tf_op jit(solution)/shard_map/gather | solution.py:222
  37.0 1.4 slice_convert_fusion.1.dcol_ref
  38.4 55.5 %all-to-all-done = bf16[128,16,768]{0,2,1:T(8,128)(2,1)} async-done(((bf16[128,16,768]{0,2,1:T(8,128)(2,1)}), bf16[128,16,768]{0,2,1:T(8,128)(2,1)}, u32[]{:S(2)}, u32[]{:S(2)}) %all-to-all-start) | async-done | bytes 3145760 | tf_op jit(solution)/shard_map/all_to_all | solution.py:256
  93.9 3.9 %copy.120 = bf16[16,128,1,768]{1,0,3,2:T(8,128)(2,1)S(1)} copy(bf16[16,128,1,768]{1,3,0,2:T(8,128)(2,1)} %bitcast.20) | data formatting | bytes 6291456 | tf_op jit(solution)/shard_map/all_to_all | solution.py:256
  99.1 1.9 slice_bitcast_fusion.3
  104.1 2.1 copy.125.k_ref
  109.3 37.5 %shard_map.129 = (bf16[2048,256]{1,0:T(8,128)(2,1)S(1)}, f32[128,2048]{1,0:T(8,128)S(1)}, f32[128,2048]{1,0:T(8,128)S(1)}, f32[4,1,256]{2,1,0:T(1,128)S(1)}) custom-call(s32[8]{0:T(128)S(1)} %and_select_fusion.lo_ref, f32[4]{0:T(128)S(1)} %pad_maximum_fusion.3.sg_ref, bf16[2048,256]{1,0:T(8,128)(2,1)S(1)} %copy.123.q_ref, ...), custom_call_target="tpu_custom_call" | custom-call | flops 6039797760 | bytes 6291456 | tf_op jit(solution)/shard_map/pallas_call | solution.py:169
  148.7 22.8 %all-to-all-start.3 = ((f32[32,2,2]{2,1,0:T(2,128)}), f32[32,2,2]{2,1,0:T(2,128)S(1)}, u32[]{:S(2)}, u32[]{:S(2)}) async-start(f32[32,2,2]{2,1,0:T(2,128)} %broadcast_in_dim.14), calls=%async_computation.3 | async-start | bytes 65536 | tf_op jit(solution)/shard_map/all_to_all | solution.py:297
  172.6 2.1 copy.127
  174.7 2.1 copy.128
  176.8 1.4 maximum_bitcast_fusion
  178.7 2.9 %reduce.10 = bf16[2048,512]{1,0:T(8,128)(2,1)} reduce(bf16[2048,1,512]{2,0,1:T(8,128)(2,1)S(1)} %maximum_bitcast_fusion, bf16[]{:T(256)} %broadcast.101), dimensions={1}, to_apply=%copy.129.reduce_sub_computation | reduce | bytes 4194306 | tf_op jit(solution)/shard_map/reshape | solution.py:284
  181.6 4.5 %reshape.213 = bf16[16,2,32768]{2,1,0:T(2,128)(2,1)} reshape(bf16[2048,512]{1,0:T(8,128)(2,1)} %reduce.10) | data formatting | bytes 4194304
  186.1 4.0 %all-to-all-start.2 = ((bf16[16,2,32768]{2,1,0:T(2,128)(2,1)}), bf16[16,2,32768]{2,1,0:T(2,128)(2,1)S(1)}, u32[]{:S(2)}, u32[]{:S(2)}) async-start(bf16[16,2,32768]{2,1,0:T(2,128)(2,1)} %reshape.213), calls=%async_computation.2 | async-start | bytes 4194304 | tf_op jit(solution)/shard_map/all_to_all | solution.py:285
  190.7 55.0 %all-to-all-done.2 = bf16[16,2,32768]{2,1,0:T(2,128)(2,1)S(1)} async-done(((bf16[16,2,32768]{2,1,0:T(2,128)(2,1)}), bf16[16,2,32768]{2,1,0:T(2,128)(2,1)S(1)}, u32[]{:S(2)}, u32[]{:S(2)}) %all-to-all-start.2) | async-done | bytes 2097184 | tf_op jit(solution)/shard_map/all_to_all | solution.py:285
  245.7 6.8 %reshape.214 = bf16[2048,1,512]{2,1,0:T(2,128)(2,1)} reshape(bf16[16,2,32768]{2,1,0:T(2,128)(2,1)S(1)} %all-to-all-done.2) | data formatting | bytes 4194304
  252.5 2.8 %copy.140 = bf16[2048,1,512]{2,0,1:T(8,128)(2,1)S(1)} copy(bf16[2048,1,512]{2,1,0:T(2,128)(2,1)} %reshape.214) | data formatting | bytes 4194304
  (73 shorter events, 22.1 us)
Async XLA Ops:
  2.4 1.1 copy-start.9
  2.4 1.1 copy-start.10
  2.5 10.5 %copy-start.6 = (bf16[1,128,4096]{2,1,0:T(8,128)(2,1)S(1)}, bf16[1,128,4096]{2,1,0:T(8,128)(2,1)}, u32[]{:S(2)}) copy-start(bf16[1,128,4096]{2,1,0:T(8,128)(2,1)} %param.14) | copy-start | bytes 3145732
  2.8 12.5 %copy-start.7 = (bf16[1,128,512]{2,1,0:T(8,128)(2,1)S(1)}, bf16[1,128,512]{2,1,0:T(8,128)(2,1)}, u32[]{:S(2)}) copy-start(bf16[1,128,512]{2,1,0:T(8,128)(2,1)} %param.11) | copy-start | bytes 393220
  2.9 12.6 %copy-start.8 = (bf16[1,128,512]{2,1,0:T(8,128)(2,1)S(1)}, bf16[1,128,512]{2,1,0:T(8,128)(2,1)}, u32[]{:S(2)}) copy-start(bf16[1,128,512]{2,1,0:T(8,128)(2,1)} %param.12) | copy-start | bytes 393220
  4.2 18.8 %all-to-all-start.1 = ((f32[128,16,4]{0,2,1:T(4,128)}), f32[128,16,4]{0,2,1:T(4,128)S(1)}, u32[]{:S(2)}, u32[]{:S(2)}) async-start(f32[128,16,4]{0,2,1:T(4,128)} %pad_maximum_fusion.1), calls=%async_computation.1 | async-start | bytes 65536 | tf_op jit(solution)/shard_map/all_to_all | solution.py:239
  17.6 9.9 %copy-start.11 = (s32[1,8]{1,0:T(1,128)S(1)}, s32[1,8]{1,0:T(1,128)}, u32[]{:S(2)}) copy-start(s32[1,8]{1,0:T(1,128)} %param.17) | copy-start | bytes 100
  17.6 17.6 %copy-start.12 = (f32[32]{0:T(128)S(1)}, f32[32]{0:T(128)}, u32[]{:S(2)}) copy-start(f32[32]{0:T(128)} %param.18) | copy-start | bytes 388
  17.6 17.6 %copy-start.13 = (f32[32]{0:T(128)S(1)}, f32[32]{0:T(128)}, u32[]{:S(2)}) copy-start(f32[32]{0:T(128)} %param.19) | copy-start | bytes 388
  23.0 70.9 %all-to-all-start = ((bf16[128,16,768]{0,2,1:T(8,128)(2,1)}), bf16[128,16,768]{0,2,1:T(8,128)(2,1)}, u32[]{:S(2)}, u32[]{:S(2)}) async-start(bf16[128,16,768]{0,2,1:T(8,128)(2,1)} %pad_maximum_fusion), calls=%async_computation | async-start | bytes 6291456 | tf_op jit(solution)/shard_map/all_to_all | solution.py:256
  35.8 62.0 %copy-start.5 = (f32[16,128,1,4]{3,1,0,2:T(8,128)}, f32[16,128,1,4]{3,1,0,2:T(8,128)S(1)}, u32[]{:S(2)}) copy-start(f32[16,128,1,4]{3,1,0,2:T(8,128)S(1)} %copy.122) | copy-start | bytes 98308
  106.2 1.0 copy-start.2
  107.2 1.0 copy-start.3
  108.2 1.0 copy-start.4
  146.8 1.0 copy-start
  147.8 29.0 %copy-start.1 = (bf16[2048,256]{1,0:T(8,128)(2,1)S(1)}, bf16[2048,256]{1,0:T(8,128)(2,1)}, u32[]{:S(2)}) copy-start(bf16[2048,256]{1,0:T(8,128)(2,1)} %copy-done) | copy-start | bytes 3145732
  148.7 37.4 %all-to-all-start.3 = ((f32[32,2,2]{2,1,0:T(2,128)}), f32[32,2,2]{2,1,0:T(2,128)S(1)}, u32[]{:S(2)}, u32[]{:S(2)}) async-start(f32[32,2,2]{2,1,0:T(2,128)} %broadcast_in_dim.14), calls=%async_computation.3 | async-start | bytes 65536 | tf_op jit(solution)/shard_map/all_to_all | solution.py:297
  186.1 59.6 %all-to-all-start.2 = ((bf16[16,2,32768]{2,1,0:T(2,128)(2,1)}), bf16[16,2,32768]{2,1,0:T(2,128)(2,1)S(1)}, u32[]{:S(2)}, u32[]{:S(2)}) async-start(bf16[16,2,32768]{2,1,0:T(2,128)(2,1)} %reshape.213), calls=%async_computation.2 | async-start | bytes 4194304 | tf_op jit(solution)/shard_map/all_to_all | solution.py:285

commit v4 on v3

v4 whole, which is shorter than its diff:
```python
import functools

import jax
import jax.numpy as jnp
from jax import lax
from jax.experimental import pallas as pl
from jax.experimental.pallas import tpu as pltpu
from jax.sharding import PartitionSpec as P

HEAD_WIDTH = 128
BLOCK = 256

masked_score = -1e30


def _grads_kernel(
    lo_ref,
    sg_ref,
    q_ref,
    do_ref,
    small_ref,
    k_ref,
    v_ref,
    dcol_ref,
    fcol_ref,
    drow_ref,
    frow_ref,
    erow_ref,
    *rest,
    hw,
    bq,
    bk,
    factor,
    head,
    accumulate,
):
    if accumulate:
        dkT_in, dvT_in = rest[:2]
        rest = rest[2:]
    dq_ref, dkT_ref, dvT_ref, bias_ref, s_scr, m_scr, l_scr, dq_scr, qT_scr, doT_scr = rest
    i = pl.program_id(0)

    @pl.when(i == 0)
    def _():
        if accumulate:
            dkT_ref[...] = dkT_in[...]
            dvT_ref[...] = dvT_in[...]
        else:
            dkT_ref[...] = jnp.zeros_like(dkT_ref)
            dvT_ref[...] = jnp.zeros_like(dvT_ref)
        bias_ref[...] = jnp.zeros_like(bias_ref)

    q0 = i * bq
    lo = lo_ref[i]
    qpos = q0 + lax.broadcasted_iota(jnp.int32, (bq, 1), 0)
    dcol = dcol_ref[...]
    fcol = fcol_ref[...]
    slope = sg_ref[0]
    gain = sg_ref[1]
    nt = (((1,), (1,)), ((), ()))

    def tile_masks(kb):
        k0 = pl.multiple_of(kb * bk, bk)
        kpos = k0 + lax.broadcasted_iota(jnp.int32, (1, bk), 1)
        drow = drow_ref[:, pl.ds(k0, bk)]
        frow = frow_ref[:, pl.ds(k0, bk)]
        erow = erow_ref[:, pl.ds(k0, bk)]
        causal = kpos <= qpos
        allowed = causal & (fcol == frow)
        anc = jnp.where(causal & (qpos < erow), 1.0, 0.0).astype(jnp.float32)
        dist = jnp.abs(dcol - drow).astype(jnp.float32)
        return k0, allowed, anc, dist

    m_scr[...] = jnp.full(m_scr.shape, masked_score, jnp.float32)
    l_scr[...] = jnp.zeros(l_scr.shape, jnp.float32)
    qT_scr[...] = q_ref[...].astype(jnp.float32).T.astype(qT_scr.dtype)
    doT_scr[...] = do_ref[...].astype(jnp.float32).T.astype(doT_scr.dtype)

    def stats(kb, carry):
        k0, allowed, anc, dist = tile_masks(kb)
        raw = lax.dot_general(q_ref[...], k_ref[pl.ds(k0, bk), :], nt, preferred_element_type=jnp.float32)
        s = raw * factor
        s = s - slope * dist + gain * anc
        s = jnp.where(allowed, s, masked_score)
        s_scr[kb] = s
        m_old = m_scr[...]
        m_new = jnp.maximum(m_old, jnp.max(s, axis=1, keepdims=True))
        l_scr[...] = l_scr[...] * jnp.exp(m_old - m_new) + jnp.sum(jnp.exp(s - m_new), axis=1, keepdims=True)
        m_scr[...] = m_new
        return carry

    lax.fori_loop(lo, i + 1, stats, 0)
    m_scr[...] = m_scr[...] + jnp.log(l_scr[...])
    dq_scr[...] = jnp.zeros(dq_scr.shape, jnp.float32)

    def grads(kb, carry):
        k0, _, anc, dist = tile_masks(kb)
        s = s_scr[kb]
        p = jnp.exp(s - m_scr[...])
        dp = lax.dot_general(do_ref[...], v_ref[pl.ds(k0, bk), :], nt, preferred_element_type=jnp.float32)
        ds = p * (dp - small_ref[:, head : head + 1])
        ds_b = ds.astype(jnp.bfloat16)
        p_b = p.astype(jnp.bfloat16)
        dq_scr[...] += jnp.dot(ds_b, k_ref[pl.ds(k0, bk), :], preferred_element_type=jnp.float32)
        dkT_ref[:, pl.ds(k0, bk)] += jnp.dot(qT_scr[...], ds_b, preferred_element_type=jnp.float32)
        dvT_ref[:, pl.ds(k0, bk)] += jnp.dot(doT_scr[...], p_b, preferred_element_type=jnp.float32)
        bias_ref[0] += jnp.sum(ds * dist, axis=0, keepdims=True)
        bias_ref[1] += jnp.sum(ds * anc, axis=0, keepdims=True)
        return carry

    lax.fori_loop(lo, i + 1, grads, 0)
    dq_ref[...] = (dq_scr[...] * factor).astype(dq_ref.dtype)


def attention_grads(
    x, q_col, do_col, kv, k_col, v_col, small, head, dcol, fcol, drow, frow, erow, lo, sg, acc=None, interpret=False
):
    seq_len, hw = kv.shape[0], HEAD_WIDTH
    bq = bk = min(BLOCK, seq_len)
    nq = seq_len // bq
    nk = seq_len // bk
    factor = hw ** (-0.5)
    accumulate = acc is not None
    kernel = functools.partial(
        _grads_kernel, hw=hw, bq=bq, bk=bk, factor=factor, head=head, accumulate=accumulate
    )
    full = lambda shape: pl.BlockSpec(shape, lambda i, lo: (0,) * len(shape))
    in_specs = [
        pl.BlockSpec(memory_space=pltpu.SMEM),
        pl.BlockSpec((bq, hw), lambda i, lo: (i, q_col)),
        pl.BlockSpec((bq, hw), lambda i, lo: (i, do_col)),
        pl.BlockSpec((bq, small.shape[1]), lambda i, lo: (i, 0)),
        pl.BlockSpec((seq_len, hw), lambda i, lo: (0, k_col)),
        pl.BlockSpec((seq_len, hw), lambda i, lo: (0, v_col)),
        pl.BlockSpec((bq, 1), lambda i, lo: (i, 0)),
        pl.BlockSpec((bq, 1), lambda i, lo: (i, 0)),
        full((1, seq_len)),
        full((1, seq_len)),
        full((1, seq_len)),
    ]
    args = [lo, sg, x, x, small, kv, kv, dcol, fcol, drow, frow, erow]
    if accumulate:
        in_specs += [full((hw, seq_len)), full((hw, seq_len))]
        args += list(acc)
    grid_spec = pltpu.PrefetchScalarGridSpec(
        num_scalar_prefetch=1,
        grid=(nq,),
        in_specs=in_specs,
        out_specs=[
            pl.BlockSpec((bq, hw), lambda i, lo: (i, 0)),
            full((hw, seq_len)),
            full((hw, seq_len)),
            full((2, 1, bk)),
        ],
        scratch_shapes=[
            pltpu.VMEM((nk, bq, bk), jnp.float32),
            pltpu.VMEM((bq, 1), jnp.float32),
            pltpu.VMEM((bq, 1), jnp.float32),
            pltpu.VMEM((bq, hw), jnp.float32),
            pltpu.VMEM((hw, bq), jnp.bfloat16),
            pltpu.VMEM((hw, bq), jnp.bfloat16),
        ],
    )
    causal_tiles = nq * (nq + 1) // 2
    flops = 2 * 5 * causal_tiles * bq * bk * hw
    return pl.pallas_call(
        kernel,
        grid_spec=grid_spec,
        out_shape=[
            jax.ShapeDtypeStruct((seq_len, hw), jnp.bfloat16),
            jax.ShapeDtypeStruct((hw, seq_len), jnp.float32),
            jax.ShapeDtypeStruct((hw, seq_len), jnp.float32),
            jax.ShapeDtypeStruct((2, 1, bk), jnp.float32),
        ],
        compiler_params=pltpu.CompilerParams(
            dimension_semantics=("arbitrary",), vmem_limit_bytes=48 * 1024 * 1024
        ),
        cost_estimate=pl.CostEstimate(
            flops=flops,
            transcendentals=2 * causal_tiles * bq * bk,
            bytes_accessed=8 * seq_len * hw,
        ),
        interpret=interpret,
    )(*args)


def body(
    queries,
    key_rows,
    values,
    outputs,
    out_grads,
    depths,
    subtree_end,
    file_lengths,
    slopes,
    ancestor_gain,
):
    tokens_here = queries.shape[1]
    context_size = lax.axis_size("ctx")
    heads_all = queries.shape[2] // HEAD_WIDTH
    kv_heads = key_rows.shape[2] // HEAD_WIDTH
    local_heads = heads_all // context_size
    group_width = heads_all // kv_heads
    repeats = context_size // kv_heads
    assert group_width // local_heads == repeats
    seq_len = tokens_here * context_size
    block = min(BLOCK, seq_len)
    factor = HEAD_WIDTH ** (-0.5)
    head_first = lax.axis_index("ctx") * local_heads
    local_slopes = lax.dynamic_slice_in_dim(slopes, head_first, local_heads)
    local_gains = lax.dynamic_slice_in_dim(ancestor_gain, head_first, local_heads)
    positions = jnp.arange(seq_len, dtype=jnp.int32)
    lengths = file_lengths[0]
    bounds = jnp.cumsum(lengths)
    starts = bounds - lengths
    file_whole = jnp.sum((positions[:, None] >= bounds[None, :]).astype(jnp.int32), axis=1)
    file_start = starts[jnp.minimum(file_whole, lengths.shape[0] - 1)]
    lo = (file_start[::block] // block).astype(jnp.int32)

    delta_tok = jnp.sum(
        (out_grads[0].astype(jnp.float32) * outputs[0].astype(jnp.float32)).reshape(
            tokens_here, heads_all, HEAD_WIDTH
        ),
        axis=2,
    )
    tree_tok = jnp.stack([depths[0], subtree_end[0]], axis=1).astype(jnp.float32)
    small_pack = jnp.concatenate(
        [
            delta_tok.reshape(tokens_here, context_size, local_heads),
            jnp.broadcast_to(tree_tok[:, None, :], (tokens_here, context_size, 2)),
        ],
        axis=2,
    )
    small_heads = lax.all_to_all(small_pack, "ctx", split_axis=1, concat_axis=0, tiled=True).reshape(
        seq_len, local_heads + 2
    )
    depth_whole = small_heads[:, local_heads].astype(jnp.int32)
    end_whole = small_heads[:, local_heads + 1].astype(jnp.int32)

    width = local_heads * HEAD_WIDTH
    query_split = queries[0].reshape(tokens_here, context_size, local_heads, HEAD_WIDTH)
    grad_split = out_grads[0].reshape(tokens_here, context_size, local_heads, HEAD_WIDTH)
    key_rep = jnp.repeat(key_rows[0].reshape(tokens_here, kv_heads, HEAD_WIDTH), repeats, axis=1)
    value_rep = jnp.repeat(values[0].reshape(tokens_here, kv_heads, HEAD_WIDTH), repeats, axis=1)
    chunks = []
    for h in range(local_heads):
        parts = [query_split[:, :, h], grad_split[:, :, h]]
        if h == 0:
            parts += [key_rep, value_rep]
        pack = jnp.concatenate(parts, axis=2)
        got = lax.all_to_all(pack, "ctx", split_axis=1, concat_axis=0, tiled=True)
        chunks.append(got.reshape(seq_len, pack.shape[2]))
    kv = chunks[0]
    tree = (
        depth_whole[:, None],
        file_whole[:, None],
        depth_whole[None, :],
        file_whole[None, :],
        end_whole[None, :],
        lo,
    )
    acc = None
    dq_back = []
    bias_rows = []
    for h in range(local_heads):
        sg = jnp.stack([local_slopes[h], local_gains[h]])
        dq_h, dkT, dvT, bias_part = attention_grads(
            chunks[h], 0, 1, kv, 2, 3, small_heads, h, *tree, sg, acc=acc
        )
        acc = (dkT, dvT)
        bias_sums = jnp.sum(bias_part, axis=(1, 2))
        bias_rows.append(jnp.stack([-bias_sums[0], bias_sums[1]]))
        if h < local_heads - 1:
            back_h = lax.all_to_all(
                dq_h.reshape(seq_len, 1, HEAD_WIDTH), "ctx", split_axis=0, concat_axis=1, tiled=True
            )
            dq_back.append(back_h)
    back_pack = jnp.concatenate(
        [dq_h, (dkT.T * factor).astype(jnp.bfloat16), dvT.T.astype(jnp.bfloat16)], axis=1
    ).reshape(seq_len, 1, 3 * HEAD_WIDTH)
    back = lax.all_to_all(back_pack, "ctx", split_axis=0, concat_axis=1, tiled=True)
    dq_back.append(back[:, :, :HEAD_WIDTH])
    query_grads = jnp.stack(dq_back, axis=2).reshape(1, tokens_here, heads_all * HEAD_WIDTH)
    key_back = back[:, :, HEAD_WIDTH : 2 * HEAD_WIDTH].astype(jnp.float32)
    value_back = back[:, :, 2 * HEAD_WIDTH :].astype(jnp.float32)
    key_grads = jnp.sum(key_back.reshape(tokens_here, kv_heads, repeats, HEAD_WIDTH), axis=2)
    value_grads = jnp.sum(value_back.reshape(tokens_here, kv_heads, repeats, HEAD_WIDTH), axis=2)
    key_grads = key_grads.astype(jnp.bfloat16).reshape(1, tokens_here, kv_heads * HEAD_WIDTH)
    value_grads = value_grads.astype(jnp.bfloat16).reshape(1, tokens_here, kv_heads * HEAD_WIDTH)
    bias_local = jnp.stack(bias_rows, axis=0)
    data_size = lax.axis_size("dp")
    bias_copies = jnp.broadcast_to(bias_local[None], (data_size, local_heads, 2))
    bias_each = lax.all_to_all(bias_copies, "dp", split_axis=0, concat_axis=0, tiled=True)
    bias_grads = jnp.sum(bias_each, axis=0)
    return (query_grads, key_grads, value_grads, bias_grads)


def solution(mesh):
    in_specs = (
        P("dp", "ctx", None),
        P("dp", "ctx", None),
        P("dp", "ctx", None),
        P("dp", "ctx", None),
        P("dp", "ctx", None),
        P("dp", "ctx"),
        P("dp", "ctx"),
        P("dp", None),
        P(),
        P(),
    )
    out_specs = (P("dp", "ctx", None), P("dp", "ctx", None), P("dp", "ctx", None), P("ctx", None))
    return jax.shard_map(body, mesh=mesh, in_specs=in_specs, out_specs=out_specs, check_vma=False)
```

time: 260 us -> 285 us (1.096)
  the two profiles are of different devices: /device:TPU:8 before, /device:TPU:6 now
where the time goes in v4:
time: 285 us; the launch traced here: 280 us
  waiting for transfers between devices  95.1 us (33%)
  starting transfers between devices  66.4 us (23%)
  Pallas kernels  49.8 us (17%)
  local copies, waits for them, and re-layouts  43.8 us (15%)
  other arithmetic  23 us (8%)
    pallas_call x2, Pallas kernels, attention_grads(): pl.pallas_call(kernel, grid_spec=grid_spec, out_shape=[jax.ShapeDtypeStru...  49.8 us
    all_to_all x2, waiting for transfers between devices, body(): got = lax.all_to_all(pack, 'ctx', split_axis=1, concat_axis=0, tiled=True)  46.4 us
    all_to_all x1, waiting for transfers between devices, body(): lax.all_to_all(back_pack, 'ctx', split_axis=0, concat_axis=1, tiled=True)  34.1 us
    unnamed x53, local copies, waits for them, and re-layouts  25.7 us
    all_to_all x1, starting transfers between devices, body(): lax.all_to_all(bias_copies, 'dp', split_axis=0, concat_axis=0, tiled=True)  23.6 us
    all_to_all x2, starting transfers between devices, body(): got = lax.all_to_all(pack, 'ctx', split_axis=1, concat_axis=0, tiled=True)  16.7 us
    all_to_all x1, starting transfers between devices, body(): lax.all_to_all(small_pack, 'ctx', split_axis=1, concat_axis=0, tiled=True)  10.1 us
    all_to_all x1, waiting for transfers between devices, body(): lax.all_to_all(dq_h.reshape(seq_len, 1, HEAD_WIDTH), 'ctx', split_axis=0,...  9.98 us
  transfers between devices with their start and end apart: 6, of which 4 were waited for; matrix products, arithmetic and copies ran while one was open for 14% of the time, Pallas kernels for 9%

profile of v4, /device:TPU:6, one launch (start us, length us, event | category | flops | bytes accessed | tf_op | source)
XLA Modules:
  0.0 280.4 jit_solution(12412446646878728519)
XLA Ops:
  0.6 1.8 multiply_bitcast_fusion
  4.2 10.1 %all-to-all-start.1 = ((f32[128,16,4]{0,2,1:T(4,128)}), f32[128,16,4]{0,2,1:T(4,128)S(1)}, u32[]{:S(2)}, u32[]{:S(2)}) async-start(f32[128,16,4]{0,2,1:T(4,128)} %pad_maximum_fusion.3), calls=%async_computation.1 | async-start | bytes 65536 | tf_op jit(solution)/shard_map/all_to_all | solution.py:235
  14.3 1.8 reshape_squeeze.13
  16.8 2.3 fusion.3
  19.1 2.5 fusion.4
  21.7 1.9 copy_bitcast_fusion.2
  23.9 1.6 pad_maximum_fusion
  25.5 9.8 %all-to-all-start = ((bf16[128,16,512]{2,0,1:T(8,128)(2,1)}), bf16[128,16,512]{2,0,1:T(8,128)(2,1)S(1)}, u32[]{:S(2)}, u32[]{:S(2)}) async-start(bf16[128,16,512]{2,0,1:T(8,128)(2,1)} %pad_maximum_fusion), calls=%async_computation | async-start | bytes 4194304 | tf_op jit(solution)/shard_map/all_to_all | solution.py:252
  36.2 1.9 copy_bitcast_fusion
  39.3 46.4 %all-to-all-done = bf16[128,16,512]{2,0,1:T(8,128)(2,1)S(1)} async-done(((bf16[128,16,512]{2,0,1:T(8,128)(2,1)}), bf16[128,16,512]{2,0,1:T(8,128)(2,1)S(1)}, u32[]{:S(2)}, u32[]{:S(2)}) %all-to-all-start) | async-done | bytes 2097184 | tf_op jit(solution)/shard_map/all_to_all | solution.py:252
  87.0 7.0 %all-to-all-start.3 = ((bf16[128,16,256]{2,0,1:T(8,128)(2,1)}), bf16[128,16,256]{2,0,1:T(8,128)(2,1)S(1)}, u32[]{:S(2)}, u32[]{:S(2)}) async-start(bf16[128,16,256]{2,0,1:T(8,128)(2,1)} %pad_maximum_fusion.1), calls=%async_computation.3 | async-start | bytes 2097152 | tf_op jit(solution)/shard_map/all_to_all | solution.py:252
  94.0 4.3 %compare_select_fusion.1 = (s32[2048,1]{0,1:T(1,128)S(1)}, s32[2048,1]{0,1:T(1,128)S(1)}) fusion(s32[]{:T(128)} %bitcast.5, s32[]{:T(128)} %bitcast.6, s32[]{:T(128)} %bitcast.7, s32[]{:T(128)} %bitcast.8, s32[]{:T(128)} %bitcast.9, s32[]{:T(128)} %bitcast.11, s32[]{:T(128)} %bitcast.10, s32[2048,1]{0,1:T(1,128)S(1)} %bitcast.84), kind=kLoop, calls=%fused_computation.23 | loop fusion | flops 32768 | bytes 24604 | tf_op jit(solution)/shard_map/gather | solution.py:218
  104.8 24.4 %shard_map.129 = (bf16[2048,128]{1,0:T(8,128)(2,1)S(1)}, f32[128,2048]{1,0:T(8,128)S(1)}, f32[128,2048]{1,0:T(8,128)S(1)}, f32[2,1,256]{2,1,0:T(1,128)S(1)}) custom-call(s32[8]{0:T(128)S(1)} %and_select_fusion.lo_ref, f32[2]{0:T(128)S(1)} %pad_maximum_fusion.5.sg_ref, bf16[2048,512]{1,0:T(8,128)(2,1)} %bitcast.92, bf16[2048,512]{1,0:T(8,128)(2,1)} %bitcast.93, ...), custom_call_target="tpu_custom_call" | custom-call | flops 3019898880 | bytes 2097152 | tf_op jit(solution)/shard_map/pallas_call | solution.py:166
  134.6 25.4 %shard_map.130 = (bf16[2048,128]{1,0:T(8,128)(2,1)S(1)}, f32[128,2048]{1,0:T(8,128)S(1)}, f32[128,2048]{1,0:T(8,128)S(1)}, f32[2,1,256]{2,1,0:T(1,128)S(1)}) custom-call(s32[8]{0:T(128)S(1)} %and_select_fusion.lo_ref, f32[2]{0:T(128)S(1)} %pad_maximum_fusion.6.sg_ref, bf16[2048,256]{1,0:T(8,128)(2,1)S(1)} %bitcast.81, bf16[2048,256]{1,0:T(8,128)(2,1)S(1)} %bitcast.82, ...), custom_call_target="tpu_custom_call" | custom-call | flops 3019898880 | bytes 2097152 | tf_op jit(solution)/shard_map/pallas_call | solution.py:166
  165.2 23.6 %all-to-all-start.5 = ((f32[32,2,2]{2,1,0:T(2,128)}), f32[32,2,2]{2,1,0:T(2,128)S(1)}, u32[]{:S(2)}, u32[]{:S(2)}) async-start(f32[32,2,2]{2,1,0:T(2,128)} %broadcast_in_dim.14), calls=%async_computation.5 | async-start | bytes 65536 | tf_op jit(solution)/shard_map/all_to_all | solution.py:294
  189.4 2.1 reduce.11
  192.3 4.6 %all-to-all-done.5 = f32[32,2,2]{2,1,0:T(2,128)S(1)} async-done(((f32[32,2,2]{2,1,0:T(2,128)}), f32[32,2,2]{2,1,0:T(2,128)S(1)}, u32[]{:S(2)}, u32[]{:S(2)}) %all-to-all-start.5) | async-done | bytes 544 | tf_op jit(solution)/shard_map/all_to_all | solution.py:294
  197.0 9.6 %all-to-all-start.2 = ((bf16[16,2,8192]{2,1,0:T(2,128)(2,1)}), bf16[16,2,8192]{2,1,0:T(2,128)(2,1)}, u32[]{:S(2)}, u32[]{:S(2)}) async-start(bf16[16,2,8192]{2,1,0:T(2,128)(2,1)} %reshape.229), calls=%async_computation.2 | async-start | bytes 1048576 | tf_op jit(solution)/shard_map/all_to_all | solution.py:275
  208.9 1.9 reduce.10
  213.1 10.0 %all-to-all-done.2 = bf16[16,2,8192]{2,1,0:T(2,128)(2,1)} async-done(((bf16[16,2,8192]{2,1,0:T(2,128)(2,1)}), bf16[16,2,8192]{2,1,0:T(2,128)(2,1)}, u32[]{:S(2)}, u32[]{:S(2)}) %all-to-all-start.2) | async-done | bytes 524320 | tf_op jit(solution)/shard_map/all_to_all | solution.py:275
  223.0 6.3 %all-to-all-start.4 = ((bf16[16,2,24576]{2,1,0:T(2,128)(2,1)}), bf16[16,2,24576]{2,1,0:T(2,128)(2,1)}, u32[]{:S(2)}, u32[]{:S(2)}) async-start(bf16[16,2,24576]{2,1,0:T(2,128)(2,1)} %reshape.227), calls=%async_computation.4 | async-start | bytes 3145728 | tf_op jit(solution)/shard_map/all_to_all | solution.py:282
  229.9 2.2 reshape.230
  233.0 34.1 %all-to-all-done.4 = bf16[16,2,24576]{2,1,0:T(2,128)(2,1)} async-done(((bf16[16,2,24576]{2,1,0:T(2,128)(2,1)}), bf16[16,2,24576]{2,1,0:T(2,128)(2,1)}, u32[]{:S(2)}, u32[]{:S(2)}) %all-to-all-start.4) | async-done | bytes 1572896 | tf_op jit(solution)/shard_map/all_to_all | solution.py:282
  267.1 8.1 %reshape.228 = bf16[2048,1,384]{2,1,0:T(2,128)(2,1)S(1)} reshape(bf16[16,2,24576]{2,1,0:T(2,128)(2,1)} %all-to-all-done.4) | data formatting | bytes 3145728
  (103 shorter events, 34.5 us)
Async XLA Ops:
  3.4 12.6 %copy-start.13 = (bf16[1,128,4096]{2,1,0:T(8,128)(2,1)S(1)}, bf16[1,128,4096]{2,1,0:T(8,128)(2,1)}, u32[]{:S(2)}) copy-start(bf16[1,128,4096]{2,1,0:T(8,128)(2,1)} %param.10) | copy-start | bytes 3145732
  4.2 21.3 %all-to-all-start.1 = ((f32[128,16,4]{0,2,1:T(4,128)}), f32[128,16,4]{0,2,1:T(4,128)S(1)}, u32[]{:S(2)}, u32[]{:S(2)}) async-start(f32[128,16,4]{0,2,1:T(4,128)} %pad_maximum_fusion.3), calls=%async_computation.1 | async-start | bytes 65536 | tf_op jit(solution)/shard_map/all_to_all | solution.py:235
  19.1 2.5 copy-start.14
  19.1 2.5 copy-start.15
  19.1 2.6 copy-start.11
  25.5 9.8 %copy-start.18 = (s32[1,8]{1,0:T(1,128)S(1)}, s32[1,8]{1,0:T(1,128)}, u32[]{:S(2)}) copy-start(s32[1,8]{1,0:T(1,128)} %param.17) | copy-start | bytes 100
  25.5 60.1 %all-to-all-start = ((bf16[128,16,512]{2,0,1:T(8,128)(2,1)}), bf16[128,16,512]{2,0,1:T(8,128)(2,1)S(1)}, u32[]{:S(2)}, u32[]{:S(2)}) async-start(bf16[128,16,512]{2,0,1:T(8,128)(2,1)} %pad_maximum_fusion), calls=%async_computation | async-start | bytes 4194304 | tf_op jit(solution)/shard_map/all_to_all | solution.py:252
  39.3 60.2 %copy-start.19 = (f32[32]{0:T(128)S(1)}, f32[32]{0:T(128)}, u32[]{:S(2)}) copy-start(f32[32]{0:T(128)} %param.18) | copy-start | bytes 388
  39.3 60.3 %copy-start.20 = (f32[32]{0:T(128)S(1)}, f32[32]{0:T(128)}, u32[]{:S(2)}) copy-start(f32[32]{0:T(128)} %param.19) | copy-start | bytes 388
  85.6 1.3 copy-start.10
  87.0 46.4 %all-to-all-start.3 = ((bf16[128,16,256]{2,0,1:T(8,128)(2,1)}), bf16[128,16,256]{2,0,1:T(8,128)(2,1)S(1)}, u32[]{:S(2)}, u32[]{:S(2)}) async-start(bf16[128,16,256]{2,0,1:T(8,128)(2,1)} %pad_maximum_fusion.1), calls=%async_computation.3 | async-start | bytes 2097152 | tf_op jit(solution)/shard_map/all_to_all | solution.py:252
  98.7 6.1 %copy-start = (s32[2048,1]{1,0:T(8,128)}, s32[2048,1]{1,0:T(8,128)S(1)}, u32[]{:S(2)}) copy-start(s32[2048,1]{1,0:T(8,128)S(1)} %copy.119.fcol_ref) | copy-start | bytes 24580
  104.8 24.4 %copy-start.1 = (s32[2048,1]{1,0:T(8,128)}, s32[2048,1]{1,0:T(8,128)S(1)}, u32[]{:S(2)}) copy-start(s32[2048,1]{1,0:T(8,128)S(1)} %slice_convert_fusion.1.dcol_ref) | copy-start | bytes 24580
  129.2 1.0 copy-start.5
  130.2 1.0 copy-start.6
  131.2 0.8 copy-start.9
  133.3 1.2 copy-start.2
  160.0 1.0 copy-start.3
  161.8 44.8 %copy-start.4 = (f32[128,2048]{1,0:T(8,128)S(1)}, f32[128,2048]{1,0:T(8,128)}, u32[]{:S(2)}) copy-start(f32[128,2048]{1,0:T(8,128)} %copy-done.3) | copy-start | bytes 3145732
  165.2 31.8 %all-to-all-start.5 = ((f32[32,2,2]{2,1,0:T(2,128)}), f32[32,2,2]{2,1,0:T(2,128)S(1)}, u32[]{:S(2)}, u32[]{:S(2)}) async-start(f32[32,2,2]{2,1,0:T(2,128)} %broadcast_in_dim.14), calls=%async_computation.5 | async-start | bytes 65536 | tf_op jit(solution)/shard_map/all_to_all | solution.py:294
  191.4 15.2 %copy-start.8 = (bf16[2048,128]{1,0:T(8,128)(2,1)S(1)}, bf16[2048,128]{1,0:T(8,128)(2,1)}, u32[]{:S(2)}) copy-start(bf16[2048,128]{1,0:T(8,128)(2,1)} %copy-done.7) | copy-start | bytes 1572868
  197.0 26.1 %all-to-all-start.2 = ((bf16[16,2,8192]{2,1,0:T(2,128)(2,1)}), bf16[16,2,8192]{2,1,0:T(2,128)(2,1)}, u32[]{:S(2)}, u32[]{:S(2)}) async-start(bf16[16,2,8192]{2,1,0:T(2,128)(2,1)} %reshape.229), calls=%async_computation.2 | async-start | bytes 1048576 | tf_op jit(solution)/shard_map/all_to_all | solution.py:275
  223.0 44.1 %all-to-all-start.4 = ((bf16[16,2,24576]{2,1,0:T(2,128)(2,1)}), bf16[16,2,24576]{2,1,0:T(2,128)(2,1)}, u32[]{:S(2)}, u32[]{:S(2)}) async-start(bf16[16,2,24576]{2,1,0:T(2,128)(2,1)} %reshape.227), calls=%async_computation.4 | async-start | bytes 3145728 | tf_op jit(solution)/shard_map/all_to_all | solution.py:282
  275.5 1.0 copy-start.12
  (3 other events, 2.2 us)

commit v5 on v3

--- a/solution.py
+++ b/solution.py
@@ -122,10 +122,11 @@
         dq_ref[:, h * hw : (h + 1) * hw] = (dq_scr[h] * factor).astype(dq_ref.dtype)
 
 
-def attention_grads(q, qT, do, doT, delta, k, kT, vT, dcol, fcol, drow, frow, erow, lo, sg, interpret=False):
-    seq_len, width = q.shape
-    hw = k.shape[1]
-    nh = width // hw
+def attention_grads(x, xT, nh, delta, dcol, fcol, drow, frow, erow, lo, sg, interpret=False):
+    seq_len = x.shape[0]
+    hw = HEAD_WIDTH
+    width = nh * hw
+    k_col = 2 * nh
     bq = bk = min(BLOCK, seq_len)
     nq = seq_len // bq
     nk = seq_len // bk
@@ -139,12 +140,12 @@
             pl.BlockSpec(memory_space=pltpu.SMEM),
             pl.BlockSpec((bq, width), lambda i, lo: (i, 0)),
             pl.BlockSpec((width, bq), lambda i, lo: (0, i)),
-            pl.BlockSpec((bq, width), lambda i, lo: (i, 0)),
-            pl.BlockSpec((width, bq), lambda i, lo: (0, i)),
+            pl.BlockSpec((bq, width), lambda i, lo: (i, 1)),
+            pl.BlockSpec((width, bq), lambda i, lo: (1, i)),
             pl.BlockSpec((bq, nh), lambda i, lo: (i, 0)),
-            full((seq_len, hw)),
-            full((hw, seq_len)),
-            full((hw, seq_len)),
+            pl.BlockSpec((seq_len, hw), lambda i, lo: (0, k_col)),
+            pl.BlockSpec((hw, seq_len), lambda i, lo: (k_col, 0)),
+            pl.BlockSpec((hw, seq_len), lambda i, lo: (k_col + 1, 0)),
             pl.BlockSpec((bq, 1), lambda i, lo: (i, 0)),
             pl.BlockSpec((bq, 1), lambda i, lo: (i, 0)),
             full((1, seq_len)),
@@ -184,7 +185,7 @@
             bytes_accessed=8 * seq_len * width + 8 * seq_len * hw,
         ),
         interpret=interpret,
-    )(lo, sg, q, qT, do, doT, delta, k, kT, vT, dcol, fcol, drow, frow, erow)
+    )(lo, sg, x, xT, x, xT, delta, x, xT, xT, dcol, fcol, drow, frow, erow)
 
 
 def body(
@@ -256,20 +257,12 @@
     big_heads = lax.all_to_all(big_pack, "ctx", split_axis=1, concat_axis=0, tiled=True).reshape(
         seq_len, 2 * width + 2 * HEAD_WIDTH
     )
-    query_heads = big_heads[:, :width]
-    grad_heads = big_heads[:, width : 2 * width]
-    key_head = big_heads[:, 2 * width : 2 * width + HEAD_WIDTH]
-    value_head = big_heads[:, 2 * width + HEAD_WIDTH :]
 
     dq, dkT, dvT, bias_part = attention_grads(
-        query_heads,
-        query_heads.T,
-        grad_heads,
-        grad_heads.T,
+        big_heads,
+        big_heads.T,
+        local_heads,
         delta_heads,
-        key_head,
-        key_head.T,
-        value_head.T,
         depth_whole[:, None],
         file_whole[:, None],
         depth_whole[None, :],

time: 260 us -> 256 us (0.985)
  local copies, waits for them, and re-layouts: 45.5 us -> 40.5 us
    reshape x0 -> x1, local copies, waits for them, and re-layouts: none -> 4.69 us  [body(): lax.all_to_all(big_pack, 'ctx', split_axis=1, concat_axis=0, tiled=True)]
    slice x3 -> x0, local copies, waits for them, and re-layouts: 3.91 us -> none  [the longest x1 2.06 us: body(): key_head = big_heads[:, 2 * width:2 * width + HEAD_WIDTH]]
    transpose x2 -> x0, local copies, waits for them, and re-layouts: 3.14 us -> none  [body(): dq, dkT, dvT, bias_part = attention_grads(query_heads, query_heads.T, gra...]
    unnamed x38 -> x32, local copies, waits for them, and re-layouts: 25 us -> 24.5 us
  transfers between devices with their start and end apart: 4 -> 4, of which waited for: 3 -> 3; matrix products, arithmetic and copies ran while one was open for 12% -> 11% of each run, Pallas kernels for 0% -> 0%
where the time goes in v5:
time: 256 us; the launch traced here: 255 us
  waiting for transfers between devices  117 us (46%)
  local copies, waits for them, and re-layouts  40.5 us (16%)
  starting transfers between devices  39.9 us (16%)
  Pallas kernels  38.1 us (15%)
  other arithmetic  18.5 us (7%)
    all_to_all x1, waiting for transfers between devices, body(): lax.all_to_all(big_pack, 'ctx', split_axis=1, concat_axis=0, tiled=True)  56.8 us
    all_to_all x1, waiting for transfers between devices, body(): lax.all_to_all(back_pack, 'ctx', split_axis=0, concat_axis=1, tiled=True)  55 us
    pallas_call x1, Pallas kernels, attention_grads(): pl.pallas_call(kernel, grid_spec=grid_spec, out_shape=[jax.ShapeDtypeStru...  38.1 us
    unnamed x32, local copies, waits for them, and re-layouts  24.5 us
    all_to_all x1, starting transfers between devices, body(): lax.all_to_all(bias_copies, 'dp', split_axis=0, concat_axis=0, tiled=True)  22.7 us
    all_to_all x1, starting transfers between devices, body(): lax.all_to_all(small_pack, 'ctx', split_axis=1, concat_axis=0, tiled=True)  8.77 us
    all_to_all x1, waiting for transfers between devices, body(): lax.all_to_all(small_pack, 'ctx', split_axis=1, concat_axis=0, tiled=True)  5.38 us
  transfers between devices with their start and end apart: 4, of which 3 were waited for; matrix products, arithmetic and copies ran while one was open for 11% of the time, Pallas kernels for 0%

profile of v5, /device:TPU:8, one launch (start us, length us, event | category | flops | bytes accessed | tf_op | source)
XLA Modules:
  0.0 255.1 jit_solution(15597560538930229271)
XLA Ops:
  0.6 1.8 multiply_bitcast_fusion
  4.2 8.8 %all-to-all-start.1 = ((f32[128,16,4]{0,2,1:T(4,128)}), f32[128,16,4]{0,2,1:T(4,128)S(1)}, u32[]{:S(2)}, u32[]{:S(2)}) async-start(f32[128,16,4]{0,2,1:T(4,128)} %pad_maximum_fusion.1), calls=%async_computation.1 | async-start | bytes 65536 | tf_op jit(solution)/shard_map/all_to_all | solution.py:240
  13.7 1.6 copy.116
  15.8 1.8 pad_maximum_fusion
  17.6 5.4 %all-to-all-done.1 = f32[128,16,4]{0,2,1:T(4,128)S(1)} async-done(((f32[128,16,4]{0,2,1:T(4,128)}), f32[128,16,4]{0,2,1:T(4,128)S(1)}, u32[]{:S(2)}, u32[]{:S(2)}) %all-to-all-start.1) | async-done | bytes 32800 | tf_op jit(solution)/shard_map/all_to_all | solution.py:240
  23.0 4.5 %all-to-all-start = ((bf16[128,16,768]{0,2,1:T(8,128)(2,1)}), bf16[128,16,768]{0,2,1:T(8,128)(2,1)}, u32[]{:S(2)}, u32[]{:S(2)}) async-start(bf16[128,16,768]{0,2,1:T(8,128)(2,1)} %pad_maximum_fusion), calls=%async_computation | async-start | bytes 6291456 | tf_op jit(solution)/shard_map/all_to_all | solution.py:257
  27.8 1.3 copy.126.fcol_ref
  29.8 4.4 %compare_select_fusion.1 = (s32[2048,1]{0,1:T(1,128)S(1)}, s32[2048,1]{0,1:T(1,128)S(1)}) fusion(s32[]{:T(128)} %bitcast.5, s32[]{:T(128)} %bitcast.6, s32[]{:T(128)} %bitcast.7, s32[]{:T(128)} %bitcast.8, s32[]{:T(128)} %bitcast.9, s32[]{:T(128)} %bitcast.11, s32[]{:T(128)} %bitcast.10, s32[2048,1]{0,1:T(1,128)S(1)} %bitcast.77), kind=kLoop, calls=%fused_computation.17 | loop fusion | flops 32768 | bytes 24604 | tf_op jit(solution)/shard_map/gather | solution.py:223
  35.6 1.2 fusion
  37.1 56.8 %all-to-all-done = bf16[128,16,768]{0,2,1:T(8,128)(2,1)} async-done(((bf16[128,16,768]{0,2,1:T(8,128)(2,1)}), bf16[128,16,768]{0,2,1:T(8,128)(2,1)}, u32[]{:S(2)}, u32[]{:S(2)}) %all-to-all-start) | async-done | bytes 3145760 | tf_op jit(solution)/shard_map/all_to_all | solution.py:257
  93.9 3.9 %copy.120 = bf16[16,128,1,768]{1,0,3,2:T(8,128)(2,1)S(1)} copy(bf16[16,128,1,768]{1,3,0,2:T(8,128)(2,1)} %bitcast.20) | data formatting | bytes 6291456 | tf_op jit(solution)/shard_map/all_to_all | solution.py:257
  97.8 3.0 %copy.147 = bf16[96,8,16,128]{3,1,2,0:T(8,128)(2,1)} copy(bf16[96,8,16,128]{3,2,1,0:T(8,128)(2,1)S(1)} %bitcast.86) | data formatting | bytes 6291456
  100.7 4.7 %copy.123.q_ref.do_ref.k_ref = bf16[2048,768]{1,0:T(8,128)(2,1)} copy(bf16[2048,768]{0,1:T(8,128)(2,1)} %bitcast.81) | data formatting | bytes 6291456 | tf_op jit(solution)/shard_map/reshape | solution.py:257
  105.4 38.1 %shard_map.129 = (bf16[2048,256]{1,0:T(8,128)(2,1)S(1)}, f32[128,2048]{1,0:T(8,128)S(1)}, f32[128,2048]{1,0:T(8,128)S(1)}, f32[4,1,256]{2,1,0:T(1,128)S(1)}) custom-call(s32[8]{0:T(128)S(1)} %and_select_fusion.lo_ref, f32[4]{0:T(128)S(1)} %pad_maximum_fusion.3.sg_ref, bf16[2048,768]{1,0:T(8,128)(2,1)} %copy.123.q_ref.do_ref.k_ref, ...), custom_call_target="tpu_custom_call" | custom-call | flops 6039797760 | bytes 6291456 | tf_op jit(solution)/shard_map/pallas_call | solution.py:170
  146.4 22.7 %all-to-all-start.3 = ((f32[32,2,2]{2,1,0:T(2,128)}), f32[32,2,2]{2,1,0:T(2,128)S(1)}, u32[]{:S(2)}, u32[]{:S(2)}) async-start(f32[32,2,2]{2,1,0:T(2,128)} %broadcast_in_dim.14), calls=%async_computation.3 | async-start | bytes 65536 | tf_op jit(solution)/shard_map/all_to_all | solution.py:290
  169.1 1.4 fusion.1
  172.6 1.4 maximum_bitcast_fusion
  174.5 2.9 %reduce.10 = bf16[2048,512]{1,0:T(8,128)(2,1)} reduce(bf16[2048,1,512]{2,0,1:T(8,128)(2,1)S(1)} %maximum_bitcast_fusion, bf16[]{:T(256)} %broadcast.101), dimensions={1}, to_apply=%copy.129.reduce_sub_computation | reduce | bytes 4194306 | tf_op jit(solution)/shard_map/reshape | solution.py:277
  177.4 4.5 %reshape.213 = bf16[16,2,32768]{2,1,0:T(2,128)(2,1)} reshape(bf16[2048,512]{1,0:T(8,128)(2,1)} %reduce.10) | data formatting | bytes 4194304
  181.9 3.9 %all-to-all-start.2 = ((bf16[16,2,32768]{2,1,0:T(2,128)(2,1)}), bf16[16,2,32768]{2,1,0:T(2,128)(2,1)S(1)}, u32[]{:S(2)}, u32[]{:S(2)}) async-start(bf16[16,2,32768]{2,1,0:T(2,128)(2,1)} %reshape.213), calls=%async_computation.2 | async-start | bytes 4194304 | tf_op jit(solution)/shard_map/all_to_all | solution.py:278
  186.5 55.0 %all-to-all-done.2 = bf16[16,2,32768]{2,1,0:T(2,128)(2,1)S(1)} async-done(((bf16[16,2,32768]{2,1,0:T(2,128)(2,1)}), bf16[16,2,32768]{2,1,0:T(2,128)(2,1)S(1)}, u32[]{:S(2)}, u32[]{:S(2)}) %all-to-all-start.2) | async-done | bytes 2097184 | tf_op jit(solution)/shard_map/all_to_all | solution.py:278
  241.5 6.8 %reshape.214 = bf16[2048,1,512]{2,1,0:T(2,128)(2,1)} reshape(bf16[16,2,32768]{2,1,0:T(2,128)(2,1)S(1)} %all-to-all-done.2) | data formatting | bytes 4194304
  248.2 2.8 %copy.140 = bf16[2048,1,512]{2,0,1:T(8,128)(2,1)S(1)} copy(bf16[2048,1,512]{2,1,0:T(2,128)(2,1)} %reshape.214) | data formatting | bytes 4194304
  251.9 1.3 copy.135
  (63 shorter events, 14.2 us)
Async XLA Ops:
  2.4 1.1 copy-start.6
  2.4 1.1 copy-start.7
  2.5 10.5 %copy-start.3 = (bf16[1,128,4096]{2,1,0:T(8,128)(2,1)S(1)}, bf16[1,128,4096]{2,1,0:T(8,128)(2,1)}, u32[]{:S(2)}) copy-start(bf16[1,128,4096]{2,1,0:T(8,128)(2,1)} %param.14) | copy-start | bytes 3145732
  2.8 12.5 %copy-start.4 = (bf16[1,128,512]{2,1,0:T(8,128)(2,1)S(1)}, bf16[1,128,512]{2,1,0:T(8,128)(2,1)}, u32[]{:S(2)}) copy-start(bf16[1,128,512]{2,1,0:T(8,128)(2,1)} %param.11) | copy-start | bytes 393220
  2.9 12.6 %copy-start.5 = (bf16[1,128,512]{2,1,0:T(8,128)(2,1)S(1)}, bf16[1,128,512]{2,1,0:T(8,128)(2,1)}, u32[]{:S(2)}) copy-start(bf16[1,128,512]{2,1,0:T(8,128)(2,1)} %param.12) | copy-start | bytes 393220
  4.2 18.8 %all-to-all-start.1 = ((f32[128,16,4]{0,2,1:T(4,128)}), f32[128,16,4]{0,2,1:T(4,128)S(1)}, u32[]{:S(2)}, u32[]{:S(2)}) async-start(f32[128,16,4]{0,2,1:T(4,128)} %pad_maximum_fusion.1), calls=%async_computation.1 | async-start | bytes 65536 | tf_op jit(solution)/shard_map/all_to_all | solution.py:240
  17.6 9.9 %copy-start.8 = (s32[1,8]{1,0:T(1,128)S(1)}, s32[1,8]{1,0:T(1,128)}, u32[]{:S(2)}) copy-start(s32[1,8]{1,0:T(1,128)} %param.17) | copy-start | bytes 100
  17.6 17.3 %copy-start.9 = (f32[32]{0:T(128)S(1)}, f32[32]{0:T(128)}, u32[]{:S(2)}) copy-start(f32[32]{0:T(128)} %param.18) | copy-start | bytes 388
  17.6 17.4 %copy-start.10 = (f32[32]{0:T(128)S(1)}, f32[32]{0:T(128)}, u32[]{:S(2)}) copy-start(f32[32]{0:T(128)} %param.19) | copy-start | bytes 388
  23.0 70.9 %all-to-all-start = ((bf16[128,16,768]{0,2,1:T(8,128)(2,1)}), bf16[128,16,768]{0,2,1:T(8,128)(2,1)}, u32[]{:S(2)}, u32[]{:S(2)}) async-start(bf16[128,16,768]{0,2,1:T(8,128)(2,1)} %pad_maximum_fusion), calls=%async_computation | async-start | bytes 6291456 | tf_op jit(solution)/shard_map/all_to_all | solution.py:257
  143.5 1.0 copy-start
  144.5 1.0 copy-start.1
  145.5 27.1 %copy-start.2 = (bf16[2048,256]{1,0:T(8,128)(2,1)S(1)}, bf16[2048,256]{1,0:T(8,128)(2,1)}, u32[]{:S(2)}) copy-start(bf16[2048,256]{1,0:T(8,128)(2,1)} %copy-done.1) | copy-start | bytes 3145732
  146.4 35.5 %all-to-all-start.3 = ((f32[32,2,2]{2,1,0:T(2,128)}), f32[32,2,2]{2,1,0:T(2,128)S(1)}, u32[]{:S(2)}, u32[]{:S(2)}) async-start(f32[32,2,2]{2,1,0:T(2,128)} %broadcast_in_dim.14), calls=%async_computation.3 | async-start | bytes 65536 | tf_op jit(solution)/shard_map/all_to_all | solution.py:290
  181.9 59.6 %all-to-all-start.2 = ((bf16[16,2,32768]{2,1,0:T(2,128)(2,1)}), bf16[16,2,32768]{2,1,0:T(2,128)(2,1)S(1)}, u32[]{:S(2)}, u32[]{:S(2)}) async-start(bf16[16,2,32768]{2,1,0:T(2,128)(2,1)} %reshape.213), calls=%async_computation.2 | async-start | bytes 4194304 | tf_op jit(solution)/shard_map/all_to_all | solution.py:278
